TPU v7x, 512 devices: a whole 4x4x16 slice. The times are simulated.
512 devices in a mesh: seg: 32 (over x, y, core), blk: 16 (over z).
Axes of the slice: x: 4, y: 4, z: 16, core: 2. Of those that a mesh axis runs over, the one named last changes fastest.
Arguments:
- spectra: bfloat16 [32, 16, 128, 4096], P('seg', 'blk'), may hold values from -6 to 6
- source_channels: int32 [16, 64], P('blk'), may hold values from 0 to 127, as said below
- pair_mask: int32 [16, 4], P('blk'), may hold values from 0 to 1, as said below
- channel_counts: int32 [16], P('blk'), may hold values from 64 to 128, as said below
Outputs:
- stacked: float32 [16, 4, 128, 1024], P('blk', None, 'seg')
Inputs may be any that keep to these rules, and one draw needn't show every extreme that they name: `channel_counts`: every block has at least 64 live channels, and some block has all 128. `source_channels`: each block's 64 sources are distinct live channels of that block. `pair_mask`: slots whose offset leads past the fibre's ends are 0.
All inputs are finite; a program needn't handle non-finite values.
Results may differ from a plain program's by a relative error of at most 0.0095.
Values may be sent and summed in bfloat16 or wider, within the bound.
No kernel may reach another device: no remote copies, remote signals or barrier semaphores. Data moves between devices by JAX's collectives and lax.ppermute only.
A program may use at most 64 MiB of HBM per device.

v0:
```python
import math

import jax
import jax.numpy as jnp
from jax import lax
from jax.sharding import PartitionSpec as P

LAGS = 16
REACH = 2


def passed_along(value, axis, by):
    devices = lax.axis_size(axis)
    pairs = [(i, i + by) for i in range(devices) if 0 <= i + by < devices]
    return lax.ppermute(value, axis, pairs)


def slot_offsets():
    return [
        slot_index - REACH if slot_index < REACH else slot_index - REACH + 1
        for slot_index in range(2 * REACH)
    ]


def make_table(bin_count, lag_count):
    freq_index = lax.broadcasted_iota(jnp.int32, (bin_count, lag_count), 0)
    lag_index = lax.broadcasted_iota(jnp.int32, (bin_count, lag_count), 1) - lag_count // 2
    turn_count = jnp.mod(freq_index * lag_index, 2 * bin_count)
    phase_angle = turn_count.astype(jnp.float32) * (math.pi / bin_count)
    scaling = 1.0 / math.sqrt(2.0 * bin_count)
    return jnp.concatenate(
        [jnp.cos(phase_angle) * scaling, -jnp.sin(phase_angle) * scaling], axis=0
    ).astype(jnp.bfloat16)


def source_kernel(sources, table):
    bin_count = table.shape[0] // 2
    source_re = sources[:, :bin_count].astype(jnp.float32).T[:, :, None]
    source_im = sources[:, bin_count:].astype(jnp.float32).T[:, :, None]
    table_re = table[:bin_count].astype(jnp.float32)[:, None, :]
    table_im = table[bin_count:].astype(jnp.float32)[:, None, :]
    upper = source_re * table_re + source_im * table_im
    lower = source_im * table_re - source_re * table_im
    joined = jnp.concatenate([upper, lower], axis=0)
    return joined.reshape(2 * bin_count, -1).astype(jnp.bfloat16)


def local(spectra, source_channels, pair_mask, channel_counts):
    own_block = spectra[0, 0]
    channels = own_block.shape[0]
    bin_count = own_block.shape[1] // 2
    lag_table = make_table(bin_count, LAGS)
    live_rows = lax.broadcasted_iota(jnp.int32, (channels, 1), 0) < channel_counts[0]
    own_block = jnp.where(live_rows, own_block, jnp.zeros_like(own_block))
    sources = jnp.take(own_block, source_channels[0], axis=0)
    weights = pair_mask[0].astype(jnp.float32)
    offsets = slot_offsets()
    term_list = []
    kernel = source_kernel(sources, lag_table)
    for slot_index, offset in enumerate(offsets):
        nearby = passed_along(own_block, "blk", -offset)
        term_list.append(
            jnp.dot(nearby, kernel, preferred_element_type=jnp.float32) * weights[slot_index]
        )
    reduced = lax.psum_scatter(jnp.stack(term_list), "seg", scatter_dimension=1, tiled=True)
    stacked = reduced * (1.0 / math.sqrt(lax.axis_size("seg")))
    return stacked[None]


def solution(mesh):
    in_specs = (P("seg", "blk", None, None), P("blk", None), P("blk", None), P("blk"))
    out_specs = P("blk", None, "seg", None)
    return jax.shard_map(local, mesh=mesh, in_specs=in_specs, out_specs=out_specs, check_vma=False)
```

profile of v0, /device:TPU:6, one launch (start us, length us, event | category | flops | bytes accessed | tf_op | source)
XLA Modules:
  0.0 249.0 jit_solution(1596429550366318412)
XLA Ops:
  7.2 1.4 bitcast_select_fusion
  8.6 6.2 %collective-permute-start = (bf16[128,4096]{1,0:T(8,128)(2,1)S(1)}, bf16[128,4096]{1,0:T(8,128)(2,1)}, u32[]{:S(2)}, u32[]{:S(2)}) collective-permute-start(bf16[128,4096]{1,0:T(8,128)(2,1)S(1)} %bitcast_select_fusion), channel_id=1, source_target_pairs={{0,2},{1,3},{2,4},{3,5},{4,6},{5,7},{6,8},{7,9},{8,10},{9,11},{10,... | collective-permute-start | bytes 3145736 | tf_op jit(solution)/shard_map/ppermute | solution.py:15
  14.7 4.8 %collective-permute-start.1 = (bf16[128,4096]{1,0:T(8,128)(2,1)S(1)}, bf16[128,4096]{1,0:T(8,128)(2,1)}, u32[]{:S(2)}, u32[]{:S(2)}) collective-permute-start(bf16[128,4096]{1,0:T(8,128)(2,1)S(1)} %bitcast_select_fusion), channel_id=1, source_target_pairs={{0,1},{1,2},{2,3},{3,4},{4,5},{5,6},{6,7},{7,8},{8,9},{9,10},{10,1... | collective-permute-start | bytes 3145736 | tf_op jit(solution)/shard_map/ppermute | solution.py:15
  19.6 1.3 collective-permute-start.2
  20.9 1.3 collective-permute-start.3
  22.2 0.7 fusion.13
  22.8 0.7 compare_and_fusion
  23.5 0.9 gather_fusion
  24.4 0.1 broadcast_select_fusion
  24.5 0.1 convert_bitcast_fusion.1
  24.6 0.7 fusion.14
  25.3 0.6 fusion.10
  25.9 2.9 %add_convert_fusion = (bf16[2048,64,16]{0,2,1:T(8,128)(2,1)S(1)}, bf16[2048,64,16]{0,2,1:T(8,128)(2,1)S(1)}) fusion(f32[2048,16]{0,1:T(8,128)S(1)} %get-tuple-element.14, f32[2048,64]{0,1:T(8,128)S(1)} %get-tuple-element.8, f32[2048,16]{0,1:T(8,128)S(1)} %get-tuple-element.13, f32[2048,64]{0,1:T(8,128)S(1)} %get-tuple-element.7), kind=kLoop, calls=%fused_computation.3 | loop fusion | flops 16777216 | bytes 9699328 | tf_op jit(solution)/shard_map/convert.5
  28.8 8.6 %collective-permute-done = bf16[128,4096]{1,0:T(8,128)(2,1)} collective-permute-done((bf16[128,4096]{1,0:T(8,128)(2,1)S(1)}, bf16[128,4096]{1,0:T(8,128)(2,1)}, u32[]{:S(2)}, u32[]{:S(2)}) %collective-permute-start) | collective-permute-done | bytes 1048608 | tf_op jit(solution)/shard_map/ppermute | solution.py:15
  37.4 4.8 %fusion.3 = f32[1,128,1024]{2,1,0:T(8,128)S(1)} fusion(bf16[128,4096]{1,0:T(8,128)(2,1)} %collective-permute-done, f32[]{:T(128)} %bitcast.9, bf16[2048,1024]{0,1:T(8,128)(2,1)S(1)} %bitcast.41, bf16[2048,1024]{0,1:T(8,128)(2,1)S(1)} %bitcast.37), kind=kOutput, calls=%fused_computation.12 | convolution fusion | flops 1090650112 | bytes 9961476 | tf_op jit(solution)/shard_map/dot_general | solution.py:63
  42.1 16.6 %collective-permute-done.1 = bf16[128,4096]{1,0:T(8,128)(2,1)} collective-permute-done((bf16[128,4096]{1,0:T(8,128)(2,1)S(1)}, bf16[128,4096]{1,0:T(8,128)(2,1)}, u32[]{:S(2)}, u32[]{:S(2)}) %collective-permute-start.1) | collective-permute-done | bytes 1048608 | tf_op jit(solution)/shard_map/ppermute | solution.py:15
  58.7 4.7 %fusion.2 = f32[1,128,1024]{2,1,0:T(8,128)S(1)} fusion(bf16[128,4096]{1,0:T(8,128)(2,1)} %collective-permute-done.1, f32[]{:T(128)} %bitcast.11, bf16[2048,1024]{0,1:T(8,128)(2,1)S(1)} %bitcast.42, bf16[2048,1024]{0,1:T(8,128)(2,1)S(1)} %bitcast.38), kind=kOutput, calls=%fused_computation.10 | convolution fusion | flops 1090650112 | bytes 9961476 | tf_op jit(solution)/shard_map/dot_general | solution.py:63
  63.4 4.7 %fusion.1 = f32[1,128,1024]{2,1,0:T(8,128)S(1)} fusion(bf16[128,4096]{1,0:T(8,128)(2,1)} %collective-permute-done.2, f32[]{:T(128)} %bitcast.13, bf16[2048,1024]{0,1:T(8,128)(2,1)S(1)} %bitcast.43, bf16[2048,1024]{0,1:T(8,128)(2,1)S(1)} %bitcast.39), kind=kOutput, calls=%fused_computation.8 | convolution fusion | flops 1090650112 | bytes 9961476 | tf_op jit(solution)/shard_map/dot_general | solution.py:63
  68.1 23.4 %collective-permute-done.3 = bf16[128,4096]{1,0:T(8,128)(2,1)S(1)} collective-permute-done((bf16[128,4096]{1,0:T(8,128)(2,1)S(1)}, bf16[128,4096]{1,0:T(8,128)(2,1)S(1)}, u32[]{:S(2)}, u32[]{:S(2)}) %collective-permute-start.3) | collective-permute-done | bytes 1048608 | tf_op jit(solution)/shard_map/ppermute | solution.py:15
  91.5 4.0 %fusion = f32[1,128,1024]{2,1,0:T(8,128)S(1)} fusion(bf16[128,4096]{1,0:T(8,128)(2,1)S(1)} %collective-permute-done.3, f32[]{:T(128)} %bitcast.15, bf16[2048,1024]{0,1:T(8,128)(2,1)S(1)} %bitcast.44, bf16[2048,1024]{0,1:T(8,128)(2,1)S(1)} %bitcast.40), kind=kOutput, calls=%fused_computation.6 | convolution fusion | flops 1090650112 | bytes 9961476 | tf_op jit(solution)/shard_map/dot_general | solution.py:63
  95.5 1.5 pad_maximum_fusion.1
  97.0 1.3 dynamic-slice
  98.9 141.7 %all-reduce.3.cloned.1.call-done = f32[4,128,1024]{2,1,0:T(8,128)} async-done(((f32[4,128,1024]{2,1,0:T(8,128)}), f32[4,128,1024]{2,1,0:T(8,128)}) %all-reduce.3.cloned.1.call-update) | async-done | bytes 2097168
  240.6 1.6 fusion.12
  (9 shorter events, 0.0 us)
Async XLA Ops:
  6.5 234.1 %all-reduce.3.cloned.1.call-start = ((), (), s32[]{:S(2)}) async-start(), calls=%async_computation | async-start | bytes 4194304
  8.6 16.0 %copy-start = (s32[1,4]{1,0:T(1,128)S(1)}, s32[1,4]{1,0:T(1,128)}, u32[]{:S(2)}) copy-start(s32[1,4]{1,0:T(1,128)} %param.6) | copy-start | bytes 52
  8.6 28.8 %collective-permute-start = (bf16[128,4096]{1,0:T(8,128)(2,1)S(1)}, bf16[128,4096]{1,0:T(8,128)(2,1)}, u32[]{:S(2)}, u32[]{:S(2)}) collective-permute-start(bf16[128,4096]{1,0:T(8,128)(2,1)S(1)} %bitcast_select_fusion), channel_id=1, source_target_pairs={{0,2},{1,3},{2,4},{3,5},{4,6},{5,7},{6,8},{7,9},{8,10},{9,11},{10,... | collective-permute-start | bytes 3145736 | tf_op jit(solution)/shard_map/ppermute | solution.py:15
  14.7 43.9 %collective-permute-start.1 = (bf16[128,4096]{1,0:T(8,128)(2,1)S(1)}, bf16[128,4096]{1,0:T(8,128)(2,1)}, u32[]{:S(2)}, u32[]{:S(2)}) collective-permute-start(bf16[128,4096]{1,0:T(8,128)(2,1)S(1)} %bitcast_select_fusion), channel_id=1, source_target_pairs={{0,1},{1,2},{2,3},{3,4},{4,5},{5,6},{6,7},{7,8},{8,9},{9,10},{10,1... | collective-permute-start | bytes 3145736 | tf_op jit(solution)/shard_map/ppermute | solution.py:15
  19.6 43.8 %collective-permute-start.2 = (bf16[128,4096]{1,0:T(8,128)(2,1)S(1)}, bf16[128,4096]{1,0:T(8,128)(2,1)}, u32[]{:S(2)}, u32[]{:S(2)}) collective-permute-start(bf16[128,4096]{1,0:T(8,128)(2,1)S(1)} %bitcast_select_fusion), channel_id=1, source_target_pairs={{1,0},{2,1},{3,2},{4,3},{5,4},{6,5},{7,6},{8,7},{9,8},{10,9},{11,1... | collective-permute-start | bytes 3145736 | tf_op jit(solution)/shard_map/ppermute | solution.py:15
  20.9 70.7 %collective-permute-start.3 = (bf16[128,4096]{1,0:T(8,128)(2,1)S(1)}, bf16[128,4096]{1,0:T(8,128)(2,1)S(1)}, u32[]{:S(2)}, u32[]{:S(2)}) collective-permute-start(bf16[128,4096]{1,0:T(8,128)(2,1)S(1)} %bitcast_select_fusion), channel_id=1, source_target_pairs={{2,0},{3,1},{4,2},{5,3},{6,4},{7,5},{8,6},{9,7},{10,8},{11,9},{12,... | collective-permute-start | bytes 3145736 | tf_op jit(solution)/shard_map/ppermute | solution.py:15
Sparse Core Ops, SparseCore 0:
  97.1 143.4 all-reduce.2
where the time goes:
time: 249 us
  waiting for transfers between devices  190 us (76%)
  matrix products  18.2 us (7%)
  between operations  14.8 us (6%)
  starting transfers between devices  13.6 us (5%)
  other arithmetic  9.4 us (4%)
  local copies, waits for them, and re-layouts  2.79 us (1%)
    unnamed x2, waiting for transfers between devices  142 us
    ppermute x4, waiting for transfers between devices, passed_along(): return lax.ppermute(value, axis, pairs)  48.5 us
    dot_general x4, matrix products, local(): jnp.dot(nearby, kernel, preferred_element_type=jnp.float32)  18.2 us
    ppermute x4, starting transfers between devices, passed_along(): return lax.ppermute(value, axis, pairs)  13.6 us
  transfers between devices with their start and end apart: 5, of which 4 were waited for; matrix products, arithmetic and copies ran while one was open for 9% of the time, Pallas kernels for 0%

commit v1 on v0

--- a/solution.py
+++ b/solution.py
@@ -6,20 +6,12 @@
 from jax.sharding import PartitionSpec as P
 
 LAGS = 16
-REACH = 2
 
 
 def passed_along(value, axis, by):
     devices = lax.axis_size(axis)
     pairs = [(i, i + by) for i in range(devices) if 0 <= i + by < devices]
     return lax.ppermute(value, axis, pairs)
-
-
-def slot_offsets():
-    return [
-        slot_index - REACH if slot_index < REACH else slot_index - REACH + 1
-        for slot_index in range(2 * REACH)
-    ]
 
 
 def make_table(bin_count, lag_count):
@@ -49,22 +41,40 @@
     own_block = spectra[0, 0]
     channels = own_block.shape[0]
     bin_count = own_block.shape[1] // 2
+    segments = lax.axis_size("seg")
+    rows = channels // segments
     lag_table = make_table(bin_count, LAGS)
     live_rows = lax.broadcasted_iota(jnp.int32, (channels, 1), 0) < channel_counts[0]
     own_block = jnp.where(live_rows, own_block, jnp.zeros_like(own_block))
-    sources = jnp.take(own_block, source_channels[0], axis=0)
-    weights = pair_mask[0].astype(jnp.float32)
-    offsets = slot_offsets()
-    term_list = []
-    kernel = source_kernel(sources, lag_table)
-    for slot_index, offset in enumerate(offsets):
-        nearby = passed_along(own_block, "blk", -offset)
-        term_list.append(
-            jnp.dot(nearby, kernel, preferred_element_type=jnp.float32) * weights[slot_index]
-        )
-    reduced = lax.psum_scatter(jnp.stack(term_list), "seg", scatter_dimension=1, tiled=True)
-    stacked = reduced * (1.0 / math.sqrt(lax.axis_size("seg")))
-    return stacked[None]
+    above = passed_along(own_block, "blk", -1)
+    below = passed_along(own_block, "blk", 1)
+    chosen = source_channels[0]
+    chosen_above = passed_along(chosen, "blk", -1)
+    chosen_below = passed_along(chosen, "blk", 1)
+
+    def kernel_of(block, channel):
+        return source_kernel(jnp.take(block, channel, axis=0), lag_table)
+
+    def product(block, kernel):
+        return jnp.dot(block, kernel, preferred_element_type=jnp.float32).astype(jnp.bfloat16)
+
+    own_kernel = kernel_of(own_block, chosen)
+    terms = jnp.stack([
+        product(below, kernel_of(above, chosen_above)),
+        product(below, own_kernel),
+        product(above, own_kernel),
+        product(above, kernel_of(below, chosen_below)),
+    ])
+    columns = terms.shape[-1]
+    pieces = terms.reshape(4, segments, rows, columns).transpose(1, 0, 2, 3)
+    pieces = pieces.reshape(segments, 4 * rows, columns)
+    received = lax.all_to_all(pieces, "seg", 0, 0, tiled=True)
+    summed = jnp.sum(received.astype(jnp.float32), axis=0).reshape(4, rows, columns)
+    moved_up = passed_along(summed[0], "blk", 1)
+    moved_down = passed_along(summed[3], "blk", -1)
+    joined = jnp.stack([moved_up, summed[1], summed[2], moved_down])
+    weights = pair_mask[0].astype(jnp.float32) * (1.0 / math.sqrt(segments))
+    return (joined * weights[:, None, None])[None]
 
 
 def solution(mesh):

time: 249 us -> 112 us (0.45)
  the two profiles are of different devices: /device:TPU:6 before, /device:TPU:96 now
where the time goes in v1:
time: 112 us; the launch traced here: 111 us
  blocking collectives  23.9 us (21%)
  matrix products  22.1 us (20%)
  other arithmetic  21.2 us (19%)
  starting transfers between devices  19.9 us (18%)
  waiting for transfers between devices  17 us (15%)
  local copies, waits for them, and re-layouts  6.37 us (6%)
    all_to_all x1, blocking collectives, local(): received = lax.all_to_all(pieces, 'seg', 0, 0, tiled=True)  23.9 us
    dot_general x4, matrix products, product(): jnp.dot(block, kernel, preferred_element_type=jnp.float32)  22.1 us
    ppermute x6, starting transfers between devices, passed_along(): return lax.ppermute(value, axis, pairs)  19.9 us
    ppermute x6, waiting for transfers between devices, passed_along(): return lax.ppermute(value, axis, pairs)  17 us
    another operation x1, other arithmetic  10.3 us
    gather x3, local copies, waits for them, and re-layouts, kernel_of(): return source_kernel(jnp.take(block, channel, axis=0), lag_table)  5.02 us
    select_n x6, other arithmetic, kernel_of(): return source_kernel(jnp.take(block, channel, axis=0), lag_table)  4.93 us
    transpose x2, other arithmetic, source_kernel(): source_re = sources[:, :bin_count].astype(jnp.float32).T[:, :, None]  2.33 us
  transfers between devices with their start and end apart: 6, of which 3 were waited for; matrix products, arithmetic and copies ran while one was open for 9% of the time, Pallas kernels for 0%

profile of v1, /device:TPU:96, one launch (start us, length us, event | category | flops | bytes accessed | tf_op | source)
XLA Modules:
  0.0 111.4 jit_solution(18128894324491162315)
XLA Ops:
  0.7 1.4 %bitcast_select_fusion = bf16[128,4096]{1,0:T(8,128)(2,1)S(1)} fusion(bf16[1,1,128,4096]{3,2,1,0:T(8,128)(2,1)} %param.6, pred[128]{0:T(512)(128)(4,1)S(1)} %iota_compare_fusion), kind=kLoop, calls=%fused_computation.26 | loop fusion | flops 524288 | bytes 2097280 | tf_op jit(solution)/shard_map/jit(_where)/select_n | solution.py:48
  2.0 5.0 %collective-permute-start = (bf16[128,4096]{1,0:T(8,128)(2,1)S(1)}, bf16[128,4096]{1,0:T(8,128)(2,1)S(1)}, u32[]{:S(2)}, u32[]{:S(2)}) collective-permute-start(bf16[128,4096]{1,0:T(8,128)(2,1)S(1)} %bitcast_select_fusion), channel_id=1, source_target_pairs={{0,1},{1,2},{2,3},{3,4},{4,5},{5,6},{6,7},{7,8},{8,9},{9,10},{10,1... | collective-permute-start | bytes 3145736 | tf_op jit(solution)/shard_map/ppermute | solution.py:14
  7.1 1.9 %collective-permute-start.1 = (bf16[128,4096]{1,0:T(8,128)(2,1)S(1)}, bf16[128,4096]{1,0:T(8,128)(2,1)S(1)}, u32[]{:S(2)}, u32[]{:S(2)}) collective-permute-start(bf16[128,4096]{1,0:T(8,128)(2,1)S(1)} %bitcast_select_fusion), channel_id=1, source_target_pairs={{1,0},{2,1},{3,2},{4,3},{5,4},{6,5},{7,6},{8,7},{9,8},{10,9},{11,1... | collective-permute-start | bytes 3145736 | tf_op jit(solution)/shard_map/ppermute | solution.py:14
  9.0 5.1 %collective-permute-start.3 = (s32[64]{0:T(128)}, s32[64]{0:T(128)S(1)}, u32[]{:S(2)}, u32[]{:S(2)}) collective-permute-start(s32[64]{0:T(128)} %bitcast.52), channel_id=1, source_target_pairs={{0,1},{1,2},{2,3},{3,4},{4,5},{5,6},{6,7},{7,8},{8,9},{9,10},{10,1... | collective-permute-start | bytes 776 | tf_op jit(solution)/shard_map/ppermute | solution.py:14
  14.2 1.9 %collective-permute-start.2 = (s32[64]{0:T(128)}, s32[64]{0:T(128)S(1)}, u32[]{:S(2)}, u32[]{:S(2)}) collective-permute-start(s32[64]{0:T(128)} %bitcast.53), channel_id=1, source_target_pairs={{1,0},{2,1},{3,2},{4,3},{5,4},{6,5},{7,6},{8,7},{9,8},{10,9},{11,1... | collective-permute-start | bytes 776 | tf_op jit(solution)/shard_map/ppermute | solution.py:14
  17.4 1.7 %gather_fusion.1 = bf16[64,4096]{1,0:T(8,128)(2,1)} fusion(bf16[128,4096]{1,0:T(8,128)(2,1)S(1)} %bitcast_select_fusion, s32[1024]{0:T(1024)S(1)} %pad_clamp_fusion.1), kind=kCustom, calls=%fused_computation.1.clone | custom fusion | bytes 1048832 | tf_op jit(solution)/shard_map/jit(_take)/gather | solution.py:56
  19.1 1.9 %broadcast_select_fusion.1 = bf16[64,4096]{1,0:T(8,128)(2,1)} fusion(bf16[64,4096]{1,0:T(8,128)(2,1)} %gather_fusion.1, pred[64]{0:T(512)(128)(4,1)S(1)} %compare_and_fusion.1), kind=kLoop, calls=%fused_computation.34 | loop fusion | flops 262144 | bytes 1048640 | tf_op jit(solution)/shard_map/jit(_take)/select_n | solution.py:56
  21.6 7.9 %collective-permute-done.3 = s32[64]{0:T(128)S(1)} collective-permute-done((s32[64]{0:T(128)}, s32[64]{0:T(128)S(1)}, u32[]{:S(2)}, u32[]{:S(2)}) %collective-permute-start.3) | collective-permute-done | bytes 288 | tf_op jit(solution)/shard_map/ppermute | solution.py:14
  29.5 5.3 %collective-permute-done.2 = s32[64]{0:T(128)S(1)} collective-permute-done((s32[64]{0:T(128)}, s32[64]{0:T(128)S(1)}, u32[]{:S(2)}, u32[]{:S(2)}) %collective-permute-start.2) | collective-permute-done | bytes 288 | tf_op jit(solution)/shard_map/ppermute | solution.py:14
  34.9 1.7 %gather_fusion = bf16[64,4096]{1,0:T(8,128)(2,1)} fusion(bf16[128,4096]{1,0:T(8,128)(2,1)S(1)} %collective-permute-done.1, s32[1024]{0:T(1024)S(1)} %pad_clamp_fusion.2), kind=kCustom, calls=%fused_computation.clone | custom fusion | bytes 1048832 | tf_op jit(solution)/shard_map/jit(_take)/gather | solution.py:56
  36.6 1.2 %broadcast_select_fusion.2 = bf16[64,4096]{1,0:T(8,128)(2,1)S(1)} fusion(bf16[64,4096]{1,0:T(8,128)(2,1)} %gather_fusion, pred[64]{0:T(512)(128)(4,1)S(1)} %compare_and_fusion.2), kind=kLoop, calls=%fused_computation.35 | loop fusion | flops 262144 | bytes 1048640 | tf_op jit(solution)/shard_map/jit(_take)/select_n | solution.py:56
  37.7 1.1 convert_bitcast_fusion.5
  38.8 1.7 %gather_fusion.2 = bf16[64,4096]{1,0:T(8,128)(2,1)} fusion(bf16[128,4096]{1,0:T(8,128)(2,1)S(1)} %collective-permute-done, s32[1024]{0:T(1024)S(1)} %pad_clamp_fusion), kind=kCustom, calls=%fused_computation.2.clone | custom fusion | bytes 1048832 | tf_op jit(solution)/shard_map/jit(_take)/gather | solution.py:56
  40.5 1.2 %broadcast_select_fusion = bf16[64,4096]{1,0:T(8,128)(2,1)S(1)} fusion(bf16[64,4096]{1,0:T(8,128)(2,1)} %gather_fusion.2, pred[64]{0:T(512)(128)(4,1)S(1)} %compare_and_fusion), kind=kLoop, calls=%fused_computation.33 | loop fusion | flops 262144 | bytes 1048640 | tf_op jit(solution)/shard_map/jit(_take)/select_n | solution.py:56
  41.7 1.3 %convert_bitcast_fusion.1 = (f32[2048,64]{0,1:T(8,128)S(1)}, f32[2048,64]{0,1:T(8,128)S(1)}, f32[2048,64]{0,1:T(8,128)S(1)}, f32[2048,64]{0,1:T(8,128)S(1)}) fusion(bf16[64,4096]{1,0:T(8,128)(2,1)S(1)} %broadcast_select_fusion, bf16[64,4096]{1,0:T(8,128)(2,1)} %broadcast_select_fusion.1), kind=kLoop, calls=%fused_computation.28 | loop fusion | flops 524288 | bytes 3145728 | tf_op jit(solution)/shard_map/transpose | solution.py:30
  43.0 10.3 %add_convert_fusion.2 = (bf16[2048,64,16]{0,2,1:T(8,128)(2,1)S(1)}, bf16[2048,64,16]{0,2,1:T(8,128)(2,1)S(1)}, bf16[2048,64,16]{0,2,1:T(8,128)(2,1)}, bf16[2048,...) fusion(f32[2048,16]{0,1:T(8,128)S(1)} %get-tuple-element.27, ...), kind=kLoop, calls=%fused_computation.17 | loop fusion | flops 50331648 | bytes 28573696 | tf_op jit(solution)/shard_map/convert.17
  53.2 3.1 %fusion.15 = bf16[128,1024]{1,0:T(8,128)(2,1)S(1)} fusion(bf16[128,4096]{1,0:T(8,128)(2,1)S(1)} %collective-permute-done, bf16[2048,1024]{0,1:T(8,128)(2,1)S(1)} %bitcast.48, bf16[2048,1024]{0,1:T(8,128)(2,1)S(1)} %bitcast.47), kind=kOutput, calls=%fused_computation.24 | convolution fusion | flops 1090650112 | bytes 9699328 | tf_op jit(solution)/shard_map/dot_general | solution.py:59
  56.5 6.3 %fusion.10 = bf16[128,1024]{1,0:T(8,128)(2,1)S(1)} fusion(bf16[128,4096]{1,0:T(8,128)(2,1)S(1)} %collective-permute-done, bf16[2048,1024]{0,1:T(8,128)(2,1)} %bitcast.43, bf16[2048,1024]{0,1:T(8,128)(2,1)} %bitcast.45), kind=kOutput, calls=%fused_computation.21 | convolution fusion | flops 1090650112 | bytes 9699328 | tf_op jit(solution)/shard_map/dot_general | solution.py:59
  63.1 6.3 %fusion.11 = bf16[128,1024]{1,0:T(8,128)(2,1)S(1)} fusion(bf16[128,4096]{1,0:T(8,128)(2,1)S(1)} %collective-permute-done.1, bf16[2048,1024]{0,1:T(8,128)(2,1)} %bitcast.44, bf16[2048,1024]{0,1:T(8,128)(2,1)} %bitcast.46), kind=kOutput, calls=%fused_computation.22 | convolution fusion | flops 1090650112 | bytes 9699328 | tf_op jit(solution)/shard_map/dot_general | solution.py:59
  69.6 6.3 %fusion.12 = bf16[128,1024]{1,0:T(8,128)(2,1)S(1)} fusion(bf16[128,4096]{1,0:T(8,128)(2,1)S(1)} %collective-permute-done.1, bf16[2048,1024]{0,1:T(8,128)(2,1)} %bitcast.41, bf16[2048,1024]{0,1:T(8,128)(2,1)} %bitcast.42), kind=kOutput, calls=%fused_computation.23 | convolution fusion | flops 1090650112 | bytes 9699328 | tf_op jit(solution)/shard_map/dot_general | solution.py:59
  76.9 23.9 %all_to_all.5 = bf16[32,16,1024]{2,1,0:T(8,128)(2,1)S(1)} all-to-all(bf16[32,16,1024]{2,1,0:T(8,128)(2,1)S(1)} %copy.19), channel_id=1, replica_groups=mesh['seg'=32,'blk'=16] {'seg'}, dimensions={0} | all-to-all | bytes 2097152 | tf_op jit(solution)/shard_map/all_to_all | solution.py:71
  101.0 2.8 %collective-permute-start.4 = (f32[4,1024]{1,0:T(4,128)S(1)}, f32[4,1024]{1,0:T(4,128)S(1)}, u32[]{:S(2)}, u32[]{:S(2)}) collective-permute-start(f32[4,1024]{1,0:T(4,128)S(1)} %get-tuple-element.22), channel_id=1, source_target_pairs={{0,1},{1,2},{2,3},{3,4},{4,5},{5,6},{6,7},{7,8},{8,9},{9,10},{10,1... | collective-permute-start | bytes 49160 | tf_op jit(solution)/shard_map/ppermute | solution.py:14
  103.8 3.0 %collective-permute-start.5 = (f32[4,1024]{1,0:T(4,128)S(1)}, f32[4,1024]{1,0:T(4,128)S(1)}, u32[]{:S(2)}, u32[]{:S(2)}) collective-permute-start(f32[4,1024]{1,0:T(4,128)S(1)} %get-tuple-element.23), channel_id=1, source_target_pairs={{1,0},{2,1},{3,2},{4,3},{5,4},{6,5},{7,6},{8,7},{9,8},{10,9},{11,1... | collective-permute-start | bytes 49160 | tf_op jit(solution)/shard_map/ppermute | solution.py:14
  106.9 3.8 %collective-permute-done.5 = f32[4,1024]{1,0:T(4,128)S(1)} collective-permute-done((f32[4,1024]{1,0:T(4,128)S(1)}, f32[4,1024]{1,0:T(4,128)S(1)}, u32[]{:S(2)}, u32[]{:S(2)}) %collective-permute-start.5) | collective-permute-done | bytes 16416 | tf_op jit(solution)/shard_map/ppermute | solution.py:14
  (35 shorter events, 4.4 us)
Async XLA Ops:
  2.0 36.8 %collective-permute-start = (bf16[128,4096]{1,0:T(8,128)(2,1)S(1)}, bf16[128,4096]{1,0:T(8,128)(2,1)S(1)}, u32[]{:S(2)}, u32[]{:S(2)}) collective-permute-start(bf16[128,4096]{1,0:T(8,128)(2,1)S(1)} %bitcast_select_fusion), channel_id=1, source_target_pairs={{0,1},{1,2},{2,3},{3,4},{4,5},{5,6},{6,7},{7,8},{8,9},{9,10},{10,1... | collective-permute-start | bytes 3145736 | tf_op jit(solution)/shard_map/ppermute | solution.py:14
  7.1 27.8 %collective-permute-start.1 = (bf16[128,4096]{1,0:T(8,128)(2,1)S(1)}, bf16[128,4096]{1,0:T(8,128)(2,1)S(1)}, u32[]{:S(2)}, u32[]{:S(2)}) collective-permute-start(bf16[128,4096]{1,0:T(8,128)(2,1)S(1)} %bitcast_select_fusion), channel_id=1, source_target_pairs={{1,0},{2,1},{3,2},{4,3},{5,4},{6,5},{7,6},{8,7},{9,8},{10,9},{11,1... | collective-permute-start | bytes 3145736 | tf_op jit(solution)/shard_map/ppermute | solution.py:14
  9.0 20.5 %collective-permute-start.3 = (s32[64]{0:T(128)}, s32[64]{0:T(128)S(1)}, u32[]{:S(2)}, u32[]{:S(2)}) collective-permute-start(s32[64]{0:T(128)} %bitcast.52), channel_id=1, source_target_pairs={{0,1},{1,2},{2,3},{3,4},{4,5},{5,6},{6,7},{7,8},{8,9},{9,10},{10,1... | collective-permute-start | bytes 776 | tf_op jit(solution)/shard_map/ppermute | solution.py:14
  14.2 20.7 %collective-permute-start.2 = (s32[64]{0:T(128)}, s32[64]{0:T(128)S(1)}, u32[]{:S(2)}, u32[]{:S(2)}) collective-permute-start(s32[64]{0:T(128)} %bitcast.53), channel_id=1, source_target_pairs={{1,0},{2,1},{3,2},{4,3},{5,4},{6,5},{7,6},{8,7},{9,8},{10,9},{11,1... | collective-permute-start | bytes 776 | tf_op jit(solution)/shard_map/ppermute | solution.py:14
  38.8 4.1 %copy-start = (f32[2048,64]{0,1:T(8,128)S(1)}, f32[2048,64]{0,1:T(8,128)}, u32[]{:S(2)}) copy-start(f32[2048,64]{0,1:T(8,128)} %get-tuple-element.12) | copy-start | bytes 1572868
  38.8 4.1 %copy-start.1 = (f32[2048,64]{0,1:T(8,128)S(1)}, f32[2048,64]{0,1:T(8,128)}, u32[]{:S(2)}) copy-start(f32[2048,64]{0,1:T(8,128)} %get-tuple-element.13) | copy-start | bytes 1572868
  76.0 30.9 %copy-start.2 = (s32[1,4]{1,0:T(1,128)S(1)}, s32[1,4]{1,0:T(1,128)}, u32[]{:S(2)}) copy-start(s32[1,4]{1,0:T(1,128)} %param.8) | copy-start | bytes 52
  101.0 5.9 %collective-permute-start.4 = (f32[4,1024]{1,0:T(4,128)S(1)}, f32[4,1024]{1,0:T(4,128)S(1)}, u32[]{:S(2)}, u32[]{:S(2)}) collective-permute-start(f32[4,1024]{1,0:T(4,128)S(1)} %get-tuple-element.22), channel_id=1, source_target_pairs={{0,1},{1,2},{2,3},{3,4},{4,5},{5,6},{6,7},{7,8},{8,9},{9,10},{10,1... | collective-permute-start | bytes 49160 | tf_op jit(solution)/shard_map/ppermute | solution.py:14
  103.8 6.8 %collective-permute-start.5 = (f32[4,1024]{1,0:T(4,128)S(1)}, f32[4,1024]{1,0:T(4,128)S(1)}, u32[]{:S(2)}, u32[]{:S(2)}) collective-permute-start(f32[4,1024]{1,0:T(4,128)S(1)} %get-tuple-element.23), channel_id=1, source_target_pairs={{1,0},{2,1},{3,2},{4,3},{5,4},{6,5},{7,6},{8,7},{9,8},{10,9},{11,1... | collective-permute-start | bytes 49160 | tf_op jit(solution)/shard_map/ppermute | solution.py:14

commit v2 on v0

v2 whole, which is shorter than its diff:
```python
import functools
import math

import jax
import jax.numpy as jnp
from jax import lax
from jax.experimental import pallas as pl
from jax.experimental.pallas import tpu as pltpu
from jax.sharding import PartitionSpec as P

LAGS = 16
CHUNKS = 2
TILE = 512
NT = (((1,), (1,)), ((), ()))


def passed_along(value, axis, by):
    devices = lax.axis_size(axis)
    pairs = [(i, i + by) for i in range(devices) if 0 <= i + by < devices]
    return lax.ppermute(value, axis, pairs)


def make_table(bin_count, lag_count):
    freq_index = lax.broadcasted_iota(jnp.int32, (lag_count, bin_count), 1)
    lag_index = lax.broadcasted_iota(jnp.int32, (lag_count, bin_count), 0) - lag_count // 2
    turn_count = jnp.mod(freq_index * lag_index, 2 * bin_count)
    phase_angle = turn_count.astype(jnp.float32) * (math.pi / bin_count)
    scaling = 1.0 / math.sqrt(2.0 * bin_count)
    return jnp.stack(
        [jnp.cos(phase_angle) * scaling, -jnp.sin(phase_angle) * scaling]
    ).astype(jnp.bfloat16)


def products_kernel(first, last, *refs):
    refs = list(refs)
    hot_above, hot_below, table, own, above, below = refs[:6]
    before = None if first else refs[6]
    out = refs[6 if first else 7]
    source_ref, kernel_ref, pair_ref = refs[-4:-1] if last else refs[-3:]
    sums = refs[-1] if last else out
    channels, half = own.shape[0], own.shape[1] // 2
    source_count, lag_count = hot_above.shape[0], table.shape[0]
    per = TILE // lag_count
    table_re = table[:, :half].astype(jnp.float32)
    table_im = table[:, half:].astype(jnp.float32)
    sides = ((hot_above, above, (below, own)), (hot_below, below, (own, above)))
    for side, (hot, near, pair) in enumerate(sides):
        source_ref[...] = jnp.dot(hot[...], near[...], preferred_element_type=jnp.float32)
        pair_ref[:channels, :] = pair[0][...]
        pair_ref[channels:, :] = pair[1][...]

        @pl.loop(0, source_count // per)
        def _(step):
            for place in range(per):
                source = step * per + place
                rows = slice(place * lag_count, (place + 1) * lag_count)
                source_re = source_ref[pl.ds(source, 1), :half]
                source_im = source_ref[pl.ds(source, 1), half:]
                upper = source_re * table_re + source_im * table_im
                lower = source_im * table_re - source_re * table_im
                kernel_ref[rows, :half] = upper.astype(jnp.bfloat16)
                kernel_ref[rows, half:] = lower.astype(jnp.bfloat16)
            rows = pl.ds(pl.multiple_of(step * TILE, TILE), TILE)
            term = lax.dot_general(
                kernel_ref[...], pair_ref[...], NT, preferred_element_type=jnp.float32
            )
            if not first:
                term = term + before[side, rows, :]
            sums[side, rows, :] = term.astype(sums.dtype)

    if last:
        segments, rows = out.shape[0], out.shape[1] // 4
        size = 2 * channels
        to = lax.broadcasted_iota(jnp.int32, (size, size), 0)
        frm = lax.broadcasted_iota(jnp.int32, (size, size), 1)
        wanted = (to // rows % 2) * channels + to // (2 * rows) * rows + to % rows
        order = (frm == wanted).astype(jnp.float32).astype(jnp.bfloat16)
        for start in range(0, source_count * lag_count, 256):
            part = slice(start, start + 256)
            halves = [
                lax.dot_general(
                    order, sums[side, part, :], NT, preferred_element_type=jnp.float32
                ).reshape(segments, 2 * rows, 256)
                for side in range(2)
            ]
            out[:, :, part] = jnp.concatenate(halves, axis=1).astype(jnp.bfloat16)


def products(hots, table, own, above, below, before, last, segments):
    channels, width = own.shape
    source_count, lag_count = hots[0].shape[0], table.shape[0]
    columns = source_count * lag_count
    first = before is None
    scratch = [
        pltpu.VMEM((source_count, width), jnp.float32),
        pltpu.VMEM((TILE, width), jnp.bfloat16),
        pltpu.VMEM((2 * channels, width), jnp.bfloat16),
    ]
    if last:
        scratch.append(pltpu.VMEM((2, columns, 2 * channels), jnp.bfloat16))
        shape = jax.ShapeDtypeStruct((segments, 4 * channels // segments, columns), jnp.bfloat16)
    else:
        shape = jax.ShapeDtypeStruct((2, columns, 2 * channels), jnp.float32)
    operands = (*hots, table, own, above, below) + (() if first else (before,))
    return pl.pallas_call(
        functools.partial(products_kernel, first, last),
        out_shape=shape,
        in_specs=[pl.BlockSpec(memory_space=pltpu.VMEM)] * len(operands),
        out_specs=pl.BlockSpec(memory_space=pltpu.VMEM),
        scratch_shapes=scratch,
        cost_estimate=pl.CostEstimate(
            flops=8 * columns * channels * width, bytes_accessed=6 * channels * width, transcendentals=0
        ),
        compiler_params=pltpu.CompilerParams(vmem_limit_bytes=32 << 20),
    )(*operands)


def local(spectra, source_channels, pair_mask, channel_counts):
    block = spectra[0, 0]
    channels, bin_count = block.shape[0], block.shape[1] // 2
    segments = lax.axis_size("seg")
    rows = channels // segments
    live_rows = lax.broadcasted_iota(jnp.int32, (channels, 1), 0) < channel_counts[0]
    part = bin_count // CHUNKS

    def chunk_of(array, index):
        re = array[..., index * part : (index + 1) * part]
        im = array[..., bin_count + index * part : bin_count + (index + 1) * part]
        return jnp.concatenate([re, im], axis=-1)

    own, above, below = [], [], []
    for index in range(CHUNKS):
        piece = chunk_of(block, index)
        piece = jnp.where(live_rows, piece, jnp.zeros_like(piece))
        own.append(piece)
        above.append(passed_along(piece, "blk", -1))
        below.append(passed_along(piece, "blk", 1))
    chosen = source_channels[0]
    channel_ids = lax.broadcasted_iota(jnp.int32, (chosen.shape[0], channels), 1)
    hots = [
        (passed_along(chosen, "blk", by)[:, None] == channel_ids).astype(jnp.bfloat16)
        for by in (-1, 1)
    ]
    table = make_table(bin_count, LAGS)
    table = jnp.concatenate([table[0], table[1]], axis=-1)
    sums = None
    for index in range(CHUNKS):
        sums = products(
            hots, chunk_of(table, index), own[index], above[index], below[index], sums, index == CHUNKS - 1, segments
        )
    received = lax.all_to_all(sums, "seg", 0, 0, tiled=True)
    summed = jnp.sum(received.astype(jnp.float32), axis=0)
    from_below = passed_along(summed[: 2 * rows], "blk", 1)
    from_above = passed_along(summed[2 * rows :], "blk", -1)
    joined = jnp.concatenate([from_below, from_above], axis=0).reshape(4, rows, -1)
    weights = pair_mask[0].astype(jnp.float32) * (1.0 / math.sqrt(segments))
    return (joined * weights[:, None, None])[None]


def solution(mesh):
    in_specs = (P("seg", "blk", None, None), P("blk", None), P("blk", None), P("blk"))
    out_specs = P("blk", None, "seg", None)
    return jax.shard_map(local, mesh=mesh, in_specs=in_specs, out_specs=out_specs, check_vma=False)
```

time: 249 us -> 76.1 us (0.31)
  the two profiles are of different devices: /device:TPU:6 before, /device:TPU:96 now
where the time goes in v2:
time: 76.1 us; the launch traced here: 75.7 us
  starting transfers between devices  28.4 us (37%)
  blocking collectives  23.9 us (31%)
  waiting for transfers between devices  11.5 us (15%)
  Pallas kernels  7.74 us (10%)
  other arithmetic  1.94 us (3%)
  local copies, waits for them, and re-layouts  1.34 us (2%)
  between operations  0.87 us (1%)
    ppermute x8, starting transfers between devices, passed_along(): return lax.ppermute(value, axis, pairs)  28.4 us
    all_to_all x1, blocking collectives, local(): received = lax.all_to_all(sums, 'seg', 0, 0, tiled=True)  23.9 us
    ppermute x8, waiting for transfers between devices, passed_along(): return lax.ppermute(value, axis, pairs)  11.5 us
    pallas_call x2, Pallas kernels, products(): pl.pallas_call(functools.partial(products_kernel, first, last), out_shape...  7.74 us
  transfers between devices with their start and end apart: 8, of which 4 were waited for; matrix products, arithmetic and copies ran while one was open for 1% of the time, Pallas kernels for 5%

profile of v2, /device:TPU:96, one launch (start us, length us, event | category | flops | bytes accessed | tf_op | source)
XLA Modules:
  0.0 75.7 jit_solution(18307272240835909118)
XLA Ops:
  0.0 1.3 %fusion.10 = (bf16[128,1024]{1,0:T(8,128)(2,1)S(1)}, bf16[128,1024]{1,0:T(8,128)(2,1)S(1)}, bf16[128,1024]{1,0:T(8,128)(2,1)S(1)}, bf16[128,1024]{1,0:T(8,128)(2,1)S(1)}) fusion(bf16[128,4096]{1,0:T(8,128)(2,1)} %bitcast.10), kind=kLoop, calls=%fused_computation.27 | loop fusion | bytes 2097152 | tf_op jit(solution)/shard_map/slice | solution.py:127
  2.0 0.3 maximum_select_fusion.1
  2.3 2.0 %collective-permute-start.4 = (bf16[128,2048]{1,0:T(8,128)(2,1)S(1)}, bf16[128,2048]{1,0:T(8,128)(2,1)S(1)}, u32[]{:S(2)}, u32[]{:S(2)}) collective-permute-start(bf16[128,2048]{1,0:T(8,128)(2,1)S(1)} %get-tuple-element.15.refs_3_), channel_id=1, source_target_pairs={{1,0},{2,1},{3,2},{4,3},{5,4},{6,5},{7,6},{8,7},{9,8},{10,9},{11,1... | collective-permute-start | bytes 1572872 | tf_op jit(solution)/shard_map/ppermute | solution.py:20
  4.3 5.0 %collective-permute-start.5 = (bf16[128,2048]{1,0:T(8,128)(2,1)S(1)}, bf16[128,2048]{1,0:T(8,128)(2,1)S(1)}, u32[]{:S(2)}, u32[]{:S(2)}) collective-permute-start(bf16[128,2048]{1,0:T(8,128)(2,1)S(1)} %get-tuple-element.15.refs_3_), channel_id=1, source_target_pairs={{0,1},{1,2},{2,3},{3,4},{4,5},{5,6},{6,7},{7,8},{8,9},{9,10},{10,1... | collective-permute-start | bytes 1572872 | tf_op jit(solution)/shard_map/ppermute | solution.py:20
  9.3 1.9 %collective-permute-start = (s32[64]{0:T(128)S(1)}, s32[64]{0:T(128)S(1)}, u32[]{:S(2)}, u32[]{:S(2)}) collective-permute-start(s32[64]{0:T(128)S(1)} %bitcast.11), channel_id=1, source_target_pairs={{1,0},{2,1},{3,2},{4,3},{5,4},{6,5},{7,6},{8,7},{9,8},{10,9},{11,1... | collective-permute-start | bytes 776 | tf_op jit(solution)/shard_map/ppermute | solution.py:20
  11.3 5.1 %collective-permute-start.1 = (s32[64]{0:T(128)S(1)}, s32[64]{0:T(128)S(1)}, u32[]{:S(2)}, u32[]{:S(2)}) collective-permute-start(s32[64]{0:T(128)S(1)} %bitcast.12), channel_id=1, source_target_pairs={{0,1},{1,2},{2,3},{3,4},{4,5},{5,6},{6,7},{7,8},{8,9},{9,10},{10,1... | collective-permute-start | bytes 776 | tf_op jit(solution)/shard_map/ppermute | solution.py:20
  16.4 1.9 %collective-permute-start.2 = (bf16[128,2048]{1,0:T(8,128)(2,1)S(1)}, bf16[128,2048]{1,0:T(8,128)(2,1)S(1)}, u32[]{:S(2)}, u32[]{:S(2)}) collective-permute-start(bf16[128,2048]{1,0:T(8,128)(2,1)S(1)} %get-tuple-element.16.refs_3_), channel_id=1, source_target_pairs={{1,0},{2,1},{3,2},{4,3},{5,4},{6,5},{7,6},{8,7},{9,8},{10,9},{11,1... | collective-permute-start | bytes 1572872 | tf_op jit(solution)/shard_map/ppermute | solution.py:20
  18.3 0.6 fusion.6
  19.0 0.3 collective-permute-done
  19.3 4.9 %collective-permute-start.3 = (bf16[128,2048]{1,0:T(8,128)(2,1)S(1)}, bf16[128,2048]{1,0:T(8,128)(2,1)S(1)}, u32[]{:S(2)}, u32[]{:S(2)}) collective-permute-start(bf16[128,2048]{1,0:T(8,128)(2,1)S(1)} %get-tuple-element.16.refs_3_), channel_id=1, source_target_pairs={{0,1},{1,2},{2,3},{3,4},{4,5},{5,6},{6,7},{7,8},{8,9},{9,10},{10,1... | collective-permute-start | bytes 1572872 | tf_op jit(solution)/shard_map/ppermute | solution.py:20
  24.2 0.1 fusion.8.refs_0_
  24.2 0.1 fusion.9.refs_1_
  24.3 0.0 collective-permute-done.4.refs_4_
  24.3 3.6 %shard_map.46.refs_6_ = f32[2,1024,256]{2,1,0:T(8,128)S(1)} custom-call(bf16[64,128]{1,0:T(8,128)(2,1)S(1)} %fusion.8.refs_0_, bf16[64,128]{1,0:T(8,128)(2,1)S(1)} %fusion.9.refs_1_, bf16[16,2048]{1,0:T(8,128)(2,1)S(1)} %pad_maximum_fusion.1.refs_2_, bf16[128,2048]{1,0:T(8,128)(2,1)S(1)} %get-tuple-element.15.refs_3_, ...), custom_call_target="tpu_custom_call" | custom-call | flops 2147483648 | bytes 1572864 | tf_op jit(solution)/shard_map/pallas_call | solution.py:105
  28.0 4.3 %collective-permute-done.2.refs_4_ = bf16[128,2048]{1,0:T(8,128)(2,1)S(1)} collective-permute-done((bf16[128,2048]{1,0:T(8,128)(2,1)S(1)}, bf16[128,2048]{1,0:T(8,128)(2,1)S(1)}, u32[]{:S(2)}, u32[]{:S(2)}) %collective-permute-start.2) | collective-permute-done | bytes 524320 | tf_op jit(solution)/shard_map/ppermute | solution.py:20
  32.2 1.9 %collective-permute-done.3.refs_5_ = bf16[128,2048]{1,0:T(8,128)(2,1)S(1)} collective-permute-done((bf16[128,2048]{1,0:T(8,128)(2,1)S(1)}, bf16[128,2048]{1,0:T(8,128)(2,1)S(1)}, u32[]{:S(2)}, u32[]{:S(2)}) %collective-permute-start.3) | collective-permute-done | bytes 524320 | tf_op jit(solution)/shard_map/ppermute | solution.py:20
  34.1 4.1 %shard_map.47 = bf16[32,16,1024]{2,1,0:T(8,128)(2,1)S(1)} custom-call(bf16[64,128]{1,0:T(8,128)(2,1)S(1)} %fusion.8.refs_0_, bf16[64,128]{1,0:T(8,128)(2,1)S(1)} %fusion.9.refs_1_, bf16[16,2048]{1,0:T(8,128)(2,1)S(1)} %pad_maximum_fusion.refs_2_, bf16[128,2048]{1,0:T(8,128)(2,1)S(1)} %get-tuple-element.16.refs_3_, ...), custom_call_target="tpu_custom_call" | custom-call | flops 2147483648 | bytes 1572864 | tf_op jit(solution)/shard_map/pallas_call | solution.py:105
  38.2 0.0 copy-start.1
  38.2 23.9 %all_to_all.5 = bf16[32,16,1024]{2,1,0:T(8,128)(2,1)S(1)} all-to-all(bf16[32,16,1024]{2,1,0:T(8,128)(2,1)S(1)} %shard_map.47), channel_id=1, replica_groups=mesh['seg'=32,'blk'=16] {'seg'}, dimensions={0} | all-to-all | bytes 2097152 | tf_op jit(solution)/shard_map/all_to_all | solution.py:151
  62.2 0.2 convert_reduce_fusion
  62.3 5.6 %collective-permute-start.6 = (f32[8,1024]{1,0:T(8,128)S(1)}, f32[8,1024]{1,0:T(8,128)S(1)}, u32[]{:S(2)}, u32[]{:S(2)}) collective-permute-start(f32[8,1024]{1,0:T(8,128)S(1)} %get-tuple-element.9), channel_id=1, source_target_pairs={{0,1},{1,2},{2,3},{3,4},{4,5},{5,6},{6,7},{7,8},{8,9},{9,10},{10,1... | collective-permute-start | bytes 98312 | tf_op jit(solution)/shard_map/ppermute | solution.py:20
  68.0 1.9 %collective-permute-start.7 = (f32[8,1024]{1,0:T(8,128)S(1)}, f32[8,1024]{1,0:T(8,128)S(1)}, u32[]{:S(2)}, u32[]{:S(2)}) collective-permute-start(f32[8,1024]{1,0:T(8,128)S(1)} %get-tuple-element.10), channel_id=1, source_target_pairs={{1,0},{2,1},{3,2},{4,3},{5,4},{6,5},{7,6},{8,7},{9,8},{10,9},{11,1... | collective-permute-start | bytes 98312 | tf_op jit(solution)/shard_map/ppermute | solution.py:20
  69.9 5.1 %collective-permute-done.7 = f32[8,1024]{1,0:T(8,128)S(1)} collective-permute-done((f32[8,1024]{1,0:T(8,128)S(1)}, f32[8,1024]{1,0:T(8,128)S(1)}, u32[]{:S(2)}, u32[]{:S(2)}) %collective-permute-start.7) | collective-permute-done | bytes 32800 | tf_op jit(solution)/shard_map/ppermute | solution.py:20
  75.0 0.7 broadcast_multiply_fusion
  (15 shorter events, 0.1 us)
Async XLA Ops:
  0.0 9.3 %copy-start = (s32[1,64]{1,0:T(1,128)S(1)}, s32[1,64]{1,0:T(1,128)}, u32[]{:S(2)}) copy-start(s32[1,64]{1,0:T(1,128)} %param.5) | copy-start | bytes 772
  2.3 22.1 %collective-permute-start.4 = (bf16[128,2048]{1,0:T(8,128)(2,1)S(1)}, bf16[128,2048]{1,0:T(8,128)(2,1)S(1)}, u32[]{:S(2)}, u32[]{:S(2)}) collective-permute-start(bf16[128,2048]{1,0:T(8,128)(2,1)S(1)} %get-tuple-element.15.refs_3_), channel_id=1, source_target_pairs={{1,0},{2,1},{3,2},{4,3},{5,4},{6,5},{7,6},{8,7},{9,8},{10,9},{11,1... | collective-permute-start | bytes 1572872 | tf_op jit(solution)/shard_map/ppermute | solution.py:20
  4.3 20.0 %collective-permute-start.5 = (bf16[128,2048]{1,0:T(8,128)(2,1)S(1)}, bf16[128,2048]{1,0:T(8,128)(2,1)S(1)}, u32[]{:S(2)}, u32[]{:S(2)}) collective-permute-start(bf16[128,2048]{1,0:T(8,128)(2,1)S(1)} %get-tuple-element.15.refs_3_), channel_id=1, source_target_pairs={{0,1},{1,2},{2,3},{3,4},{4,5},{5,6},{6,7},{7,8},{8,9},{9,10},{10,1... | collective-permute-start | bytes 1572872 | tf_op jit(solution)/shard_map/ppermute | solution.py:20
  9.3 9.9 %collective-permute-start = (s32[64]{0:T(128)S(1)}, s32[64]{0:T(128)S(1)}, u32[]{:S(2)}, u32[]{:S(2)}) collective-permute-start(s32[64]{0:T(128)S(1)} %bitcast.11), channel_id=1, source_target_pairs={{1,0},{2,1},{3,2},{4,3},{5,4},{6,5},{7,6},{8,7},{9,8},{10,9},{11,1... | collective-permute-start | bytes 776 | tf_op jit(solution)/shard_map/ppermute | solution.py:20
  11.3 13.0 %collective-permute-start.1 = (s32[64]{0:T(128)S(1)}, s32[64]{0:T(128)S(1)}, u32[]{:S(2)}, u32[]{:S(2)}) collective-permute-start(s32[64]{0:T(128)S(1)} %bitcast.12), channel_id=1, source_target_pairs={{0,1},{1,2},{2,3},{3,4},{4,5},{5,6},{6,7},{7,8},{8,9},{9,10},{10,1... | collective-permute-start | bytes 776 | tf_op jit(solution)/shard_map/ppermute | solution.py:20
  16.4 15.8 %collective-permute-start.2 = (bf16[128,2048]{1,0:T(8,128)(2,1)S(1)}, bf16[128,2048]{1,0:T(8,128)(2,1)S(1)}, u32[]{:S(2)}, u32[]{:S(2)}) collective-permute-start(bf16[128,2048]{1,0:T(8,128)(2,1)S(1)} %get-tuple-element.16.refs_3_), channel_id=1, source_target_pairs={{1,0},{2,1},{3,2},{4,3},{5,4},{6,5},{7,6},{8,7},{9,8},{10,9},{11,1... | collective-permute-start | bytes 1572872 | tf_op jit(solution)/shard_map/ppermute | solution.py:20
  19.3 14.8 %collective-permute-start.3 = (bf16[128,2048]{1,0:T(8,128)(2,1)S(1)}, bf16[128,2048]{1,0:T(8,128)(2,1)S(1)}, u32[]{:S(2)}, u32[]{:S(2)}) collective-permute-start(bf16[128,2048]{1,0:T(8,128)(2,1)S(1)} %get-tuple-element.16.refs_3_), channel_id=1, source_target_pairs={{0,1},{1,2},{2,3},{3,4},{4,5},{5,6},{6,7},{7,8},{8,9},{9,10},{10,1... | collective-permute-start | bytes 1572872 | tf_op jit(solution)/shard_map/ppermute | solution.py:20
  38.2 31.7 %copy-start.1 = (s32[1,4]{1,0:T(1,128)S(1)}, s32[1,4]{1,0:T(1,128)}, u32[]{:S(2)}) copy-start(s32[1,4]{1,0:T(1,128)} %param.6) | copy-start | bytes 52
  62.3 7.6 %collective-permute-start.6 = (f32[8,1024]{1,0:T(8,128)S(1)}, f32[8,1024]{1,0:T(8,128)S(1)}, u32[]{:S(2)}, u32[]{:S(2)}) collective-permute-start(f32[8,1024]{1,0:T(8,128)S(1)} %get-tuple-element.9), channel_id=1, source_target_pairs={{0,1},{1,2},{2,3},{3,4},{4,5},{5,6},{6,7},{7,8},{8,9},{9,10},{10,1... | collective-permute-start | bytes 98312 | tf_op jit(solution)/shard_map/ppermute | solution.py:20
  68.0 7.0 %collective-permute-start.7 = (f32[8,1024]{1,0:T(8,128)S(1)}, f32[8,1024]{1,0:T(8,128)S(1)}, u32[]{:S(2)}, u32[]{:S(2)}) collective-permute-start(f32[8,1024]{1,0:T(8,128)S(1)} %get-tuple-element.10), channel_id=1, source_target_pairs={{1,0},{2,1},{3,2},{4,3},{5,4},{6,5},{7,6},{8,7},{9,8},{10,9},{11,1... | collective-permute-start | bytes 98312 | tf_op jit(solution)/shard_map/ppermute | solution.py:20

commit v3 on v2

v3 whole, which is shorter than its diff:
```python
import functools
import math

import jax
import jax.numpy as jnp
from jax import lax
from jax.experimental import pallas as pl
from jax.experimental.pallas import tpu as pltpu
from jax.sharding import PartitionSpec as P

LAGS = 16
CHUNKS = (5, 3)
TILE = 512
TAG = 128
NT = (((1,), (1,)), ((), ()))
TN = (((0,), (0,)), ((), ()))


def passed_along(value, by):
    segments, blocks = lax.axis_size("seg"), lax.axis_size("blk")
    pairs = []
    for segment in range(segments):
        step = by if segment % 2 == 0 else -by
        for block in range(blocks):
            if 0 <= block + step < blocks:
                pairs.append((segment * blocks + block, segment * blocks + block + step))
    return lax.ppermute(value, ("seg", "blk"), pairs)


def to_other_core(value):
    return lax.ppermute(value, "seg", [(i, i ^ 1) for i in range(lax.axis_size("seg"))])


def make_table(bin_count, lag_count):
    freq_index = lax.broadcasted_iota(jnp.int32, (lag_count, bin_count), 1)
    lag_index = lax.broadcasted_iota(jnp.int32, (lag_count, bin_count), 0) - lag_count // 2
    turn_count = jnp.mod(freq_index * lag_index, 2 * bin_count)
    phase_angle = turn_count.astype(jnp.float32) * (math.pi / bin_count)
    scaling = 1.0 / math.sqrt(2.0 * bin_count)
    return jnp.stack(
        [jnp.cos(phase_angle) * scaling, -jnp.sin(phase_angle) * scaling]
    ).astype(jnp.bfloat16)


def products_kernel(first, last, *refs):
    refs = list(refs)
    tag, table, own, near, far = refs[:5]
    before = None if first else refs[5]
    out = refs[5 if first else 6]
    source_ref, kernel_ref, pair_ref = refs[-4:-1] if last else refs[-3:]
    sums = refs[-1] if last else out
    channels, half = own.shape[0], table.shape[1] // 2
    source_count, lag_count = source_ref.shape[0], table.shape[0]
    per = TILE // lag_count
    table_re = table[:, :half].astype(jnp.float32)
    table_im = table[:, half:].astype(jnp.float32)
    hot = tag[:, tag.shape[1] - TAG :]
    picked = lax.dot_general(hot, near[:, : 2 * half], TN, preferred_element_type=jnp.float32)
    source_ref[...] = picked[:source_count]
    pair_ref[:channels, :] = far[:, : 2 * half]
    pair_ref[channels:, :] = own[:, : 2 * half]

    @pl.loop(0, source_count // per)
    def _(step):
        for place in range(per):
            source = step * per + place
            rows = slice(place * lag_count, (place + 1) * lag_count)
            source_re = source_ref[pl.ds(source, 1), :half]
            source_im = source_ref[pl.ds(source, 1), half:]
            upper = source_re * table_re + source_im * table_im
            lower = source_im * table_re - source_re * table_im
            kernel_ref[rows, :half] = upper.astype(jnp.bfloat16)
            kernel_ref[rows, half:] = lower.astype(jnp.bfloat16)
        rows = pl.ds(pl.multiple_of(step * TILE, TILE), TILE)
        term = lax.dot_general(
            kernel_ref[...], pair_ref[...], NT, preferred_element_type=jnp.float32
        )
        if not first:
            term = term + before[rows, :]
        sums[rows, :] = term.astype(sums.dtype)

    if last:
        chips, rows = out.shape[0], out.shape[1] // 2
        size = 2 * channels
        to = lax.broadcasted_iota(jnp.int32, (size, size), 0)
        frm = lax.broadcasted_iota(jnp.int32, (size, size), 1)
        wanted = to // rows % 2 * channels + to // (2 * rows) * rows + to % rows
        order = (frm == wanted).astype(jnp.float32).astype(jnp.bfloat16)
        for start in range(0, source_count * lag_count, 256):
            part = slice(start, start + 256)
            turned = lax.dot_general(order, sums[part, :], NT, preferred_element_type=jnp.float32)
            out[:, :, part] = turned.reshape(chips, 2 * rows, 256).astype(jnp.bfloat16)


def products(tag, source_count, table, own, near, far, before, last, chips):
    channels, (lag_count, width) = own.shape[0], table.shape
    columns = source_count * lag_count
    first = before is None
    scratch = [
        pltpu.VMEM((source_count, width), jnp.float32),
        pltpu.VMEM((TILE, width), jnp.bfloat16),
        pltpu.VMEM((2 * channels, width), jnp.bfloat16),
    ]
    if last:
        scratch.append(pltpu.VMEM((columns, 2 * channels), jnp.bfloat16))
        shape = jax.ShapeDtypeStruct((chips, 2 * channels // chips, columns), jnp.bfloat16)
    else:
        shape = jax.ShapeDtypeStruct((columns, 2 * channels), jnp.float32)
    operands = (tag, table, own, near, far) + (() if first else (before,))
    return pl.pallas_call(
        functools.partial(products_kernel, first, last),
        out_shape=shape,
        in_specs=[pl.BlockSpec(memory_space=pltpu.VMEM)] * len(operands),
        out_specs=pl.BlockSpec(memory_space=pltpu.VMEM),
        scratch_shapes=scratch,
        cost_estimate=pl.CostEstimate(
            flops=4 * columns * channels * width, bytes_accessed=6 * channels * width, transcendentals=0
        ),
        compiler_params=pltpu.CompilerParams(vmem_limit_bytes=24 << 20),
    )(*operands)


def local(spectra, source_channels, pair_mask, channel_counts):
    block = spectra[0, 0]
    channels, bin_count = block.shape[0], block.shape[1] // 2
    segments = lax.axis_size("seg")
    chips, rows = segments // 2, channels // segments
    live_rows = lax.broadcasted_iota(jnp.int32, (channels, 1), 0) < channel_counts[0]
    parts = [bin_count * share // sum(CHUNKS) for share in CHUNKS]
    starts = [sum(parts[:index]) for index in range(len(parts))]

    def chunk_of(array, index):
        bins = slice(starts[index], starts[index] + parts[index])
        re, im = array[..., :bin_count], array[..., bin_count:]
        return jnp.concatenate([re[..., bins], im[..., bins]], axis=-1)

    chosen = jnp.pad(source_channels[0], (0, TAG - source_channels.shape[1]), constant_values=channels)
    channel_ids = lax.broadcasted_iota(jnp.int32, (channels, TAG), 0)
    hot = jnp.logical_and(chosen[None, :] == channel_ids, live_rows).astype(jnp.bfloat16)
    own, one, other = [], [], []
    for index in range(len(parts)):
        piece = chunk_of(block, index)
        piece = jnp.where(live_rows, piece, jnp.zeros_like(piece))
        if index == 0:
            piece = jnp.concatenate([piece, hot], axis=1)
        own.append(piece)
        one.append(passed_along(piece, 1))
        other.append(passed_along(piece, -1))
        block, _ = lax.optimization_barrier((block, piece))
    table = make_table(bin_count, LAGS)
    table = jnp.concatenate([table[0], table[1]], axis=-1)
    sources = source_channels.shape[1]

    def side(near, far, sums, index):
        last = index == len(parts) - 1
        return products(
            near[0], sources, chunk_of(table, index), own[index], near[index], far[index], sums, last, chips
        )

    given, kept = None, None
    for index in range(len(parts)):
        given = side(other, one, given, index)
        kept = side(one, other, kept, index)
        if index < len(parts) - 1:
            given, kept = lax.optimization_barrier((given, kept))
    taken = to_other_core(given)
    both = (kept.astype(jnp.float32) + taken.astype(jnp.float32)).astype(jnp.bfloat16)
    groups = [list(range(start, segments, 2)) for start in range(2)]
    received = lax.all_to_all(both, "seg", 0, 0, axis_index_groups=groups, tiled=True)
    summed = jnp.sum(received.astype(jnp.float32), axis=0)
    arrived = passed_along(summed, -1).reshape(2, 2, rows, -1)
    first_core = lax.axis_index("seg") % 2 == 0
    mine = jnp.where(first_core, arrived[:, 0], arrived[:, 1])
    theirs = to_other_core(jnp.where(first_core, arrived[:, 1], arrived[:, 0]))
    lower = jnp.where(first_core, theirs, mine)
    upper = jnp.where(first_core, mine, theirs)
    joined = jnp.concatenate([lower, upper[::-1]], axis=0)
    weights = pair_mask[0].astype(jnp.float32) * (1.0 / math.sqrt(segments))
    return (joined * weights[:, None, None])[None]


def solution(mesh):
    in_specs = (P("seg", "blk", None, None), P("blk", None), P("blk", None), P("blk"))
    out_specs = P("blk", None, "seg", None)
    return jax.shard_map(local, mesh=mesh, in_specs=in_specs, out_specs=out_specs, check_vma=False)
```

time: 76.1 us -> 68.1 us (0.89)
  starting transfers between devices: 28.4 us -> 20.1 us
  blocking collectives: 23.9 us -> 18.7 us
  waiting for transfers between devices: 11.5 us -> 15.3 us
  local copies, waits for them, and re-layouts: 1.34 us -> 2.24 us
    ppermute x8 -> x7, starting transfers between devices: 28.4 us -> 20.1 us  [the longest x5 15.9 us: passed_along(): return lax.ppermute(value, ('seg', 'blk'), pairs)]
    all_to_all x1, blocking collectives: 23.9 us -> 18.7 us  [local(): lax.all_to_all(both, 'seg', 0, 0, axis_index_groups=groups, tiled=True)]
    ppermute x8 -> x7, waiting for transfers between devices: 11.5 us -> 15.3 us  [the longest x5 14.2 us: passed_along(): return lax.ppermute(value, ('seg', 'blk'), pairs)]
    slice x3 -> x6, local copies, waits for them, and re-layouts: 1.31 us -> 2.2 us  [chunk_of(): return jnp.concatenate([re[..., bins], im[..., bins]], axis=-1)]
    pallas_call x2 -> x4, Pallas kernels: 7.74 us -> 8.04 us  [products(): pl.pallas_call(functools.partial(products_kernel, first, last), out_shape...]
  transfers between devices with their start and end apart: 8 -> 7, of which waited for: 4 -> 4; matrix products, arithmetic and copies ran while one was open for 1% -> 3% of each run, Pallas kernels for 5% -> 9%
where the time goes in v3:
time: 68.1 us; the launch traced here: 67.4 us
  starting transfers between devices  20.1 us (30%)
  blocking collectives  18.7 us (27%)
  waiting for transfers between devices  15.3 us (22%)
  Pallas kernels  8.04 us (12%)
  local copies, waits for them, and re-layouts  2.24 us (3%)
  other arithmetic  2.09 us (3%)
  between operations  0.94 us (1%)
    all_to_all x1, blocking collectives, local(): lax.all_to_all(both, 'seg', 0, 0, axis_index_groups=groups, tiled=True)  18.7 us
    ppermute x5, starting transfers between devices, passed_along(): return lax.ppermute(value, ('seg', 'blk'), pairs)  15.9 us
    ppermute x5, waiting for transfers between devices, passed_along(): return lax.ppermute(value, ('seg', 'blk'), pairs)  14.2 us
    pallas_call x4, Pallas kernels, products(): pl.pallas_call(functools.partial(products_kernel, first, last), out_shape...  8.04 us
    ppermute x2, starting transfers between devices, to_other_core(): lax.ppermute(value, 'seg', [(i, i ^ 1) for i in range(lax.axis_size('seg'...  4.2 us
    slice x6, local copies, waits for them, and re-layouts, chunk_of(): return jnp.concatenate([re[..., bins], im[..., bins]], axis=-1)  2.2 us
  transfers between devices with their start and end apart: 7, of which 4 were waited for; matrix products, arithmetic and copies ran while one was open for 3% of the time, Pallas kernels for 9%

profile of v3, /device:TPU:96, one launch (start us, length us, event | category | flops | bytes accessed | tf_op | source)
XLA Modules:
  0.0 67.4 jit_solution(17610832806997264660)
XLA Ops:
  0.0 1.1 %fusion.13 = (bf16[128,1280]{1,0:T(8,128)(2,1)S(1)}, bf16[128,1280]{1,0:T(8,128)(2,1)S(1)}) fusion(bf16[128,4096]{1,0:T(8,128)(2,1)} %bitcast.35), kind=kLoop, calls=%fused_computation.35 | loop fusion | bytes 1310720 | tf_op jit(solution)/shard_map/slice | solution.py:135
  1.8 0.1 fusion.9
  1.9 0.2 maximum_select_fusion
  2.1 5.0 %collective-permute-start = (bf16[128,2688]{1,0:T(8,128)(2,1)S(1)}, bf16[128,2688]{1,0:T(8,128)(2,1)S(1)}, u32[]{:S(2)}, u32[]{:S(2)}) collective-permute-start(bf16[128,2688]{1,0:T(8,128)(2,1)S(1)} %pad_maximum_fusion.refs_2_), channel_id=1, source_target_pairs={{0,1},{1,2},{2,3},{3,4},{4,5},{5,6},{6,7},{7,8},{8,9},{9,10},{10,1... | collective-permute-start | bytes 2064392 | tf_op jit(solution)/shard_map/ppermute | solution.py:27
  7.2 1.9 %collective-permute-start.3 = (bf16[128,2688]{1,0:T(8,128)(2,1)S(1)}, bf16[128,2688]{1,0:T(8,128)(2,1)S(1)}, u32[]{:S(2)}, u32[]{:S(2)}) collective-permute-start(bf16[128,2688]{1,0:T(8,128)(2,1)S(1)} %pad_maximum_fusion.refs_2_), channel_id=1, source_target_pairs={{1,0},{2,1},{3,2},{4,3},{5,4},{6,5},{7,6},{8,7},{9,8},{10,9},{11,1... | collective-permute-start | bytes 2064392 | tf_op jit(solution)/shard_map/ppermute | solution.py:27
  9.1 1.1 %fusion.12 = (bf16[128,768]{1,0:T(8,128)(2,1)S(1)}, bf16[128,768]{1,0:T(8,128)(2,1)S(1)}) fusion(bf16[128,4096]{1,0:T(8,128)(2,1)} %bitcast.36), kind=kLoop, calls=%fused_computation.34 | loop fusion | bytes 786432 | tf_op jit(solution)/shard_map/slice | solution.py:135
  10.2 0.1 maximum_select_fusion.1.refs_2_
  10.3 5.1 %collective-permute-start.1 = (bf16[128,1536]{1,0:T(8,128)(2,1)S(1)}, bf16[128,1536]{1,0:T(8,128)(2,1)S(1)}, u32[]{:S(2)}, u32[]{:S(2)}) collective-permute-start(bf16[128,1536]{1,0:T(8,128)(2,1)S(1)} %maximum_select_fusion.1.refs_2_), channel_id=1, source_target_pairs={{0,1},{1,2},{2,3},{3,4},{4,5},{5,6},{6,7},{7,8},{8,9},{9,10},{10,1... | collective-permute-start | bytes 1179656 | tf_op jit(solution)/shard_map/ppermute | solution.py:27
  15.5 1.9 %collective-permute-start.2 = (bf16[128,1536]{1,0:T(8,128)(2,1)S(1)}, bf16[128,1536]{1,0:T(8,128)(2,1)S(1)}, u32[]{:S(2)}, u32[]{:S(2)}) collective-permute-start(bf16[128,1536]{1,0:T(8,128)(2,1)S(1)} %maximum_select_fusion.1.refs_2_), channel_id=1, source_target_pairs={{1,0},{2,1},{3,2},{4,3},{5,4},{6,5},{7,6},{8,7},{9,8},{10,9},{11,1... | collective-permute-start | bytes 1179656 | tf_op jit(solution)/shard_map/ppermute | solution.py:27
  17.4 0.6 fusion.6
  18.1 4.2 %collective-permute-done.refs_4_.refs_0_.refs_3_ = bf16[128,2688]{1,0:T(8,128)(2,1)S(1)} collective-permute-done((bf16[128,2688]{1,0:T(8,128)(2,1)S(1)}, bf16[128,2688]{1,0:T(8,128)(2,1)S(1)}, u32[]{:S(2)}, u32[]{:S(2)}) %collective-permute-start) | collective-permute-done | bytes 688160 | tf_op jit(solution)/shard_map/ppermute | solution.py:27
  22.2 4.6 %collective-permute-done.3.refs_0_.refs_3_.refs_4_ = bf16[128,2688]{1,0:T(8,128)(2,1)S(1)} collective-permute-done((bf16[128,2688]{1,0:T(8,128)(2,1)S(1)}, bf16[128,2688]{1,0:T(8,128)(2,1)S(1)}, u32[]{:S(2)}, u32[]{:S(2)}) %collective-permute-start.3) | collective-permute-done | bytes 688160 | tf_op jit(solution)/shard_map/ppermute | solution.py:27
  26.8 2.2 %shard_map.47.refs_5_ = f32[1024,256]{1,0:T(8,128)S(1)} custom-call(bf16[128,2688]{1,0:T(8,128)(2,1)S(1)} %collective-permute-done.refs_4_.refs_0_.refs_3_, bf16[16,2560]{1,0:T(8,128)(2,1)S(1)} %pad_maximum_fusion.1.refs_1_, bf16[128,2688]{1,0:T(8,128)(2,1)S(1)} %pad_maximum_fusion.refs_2_, ...), custom_call_target="tpu_custom_call" | custom-call | flops 1342177280 | bytes 1966080 | tf_op jit(solution)/shard_map/pallas_call | solution.py:110
  29.0 2.1 %shard_map.46.refs_5_ = f32[1024,256]{1,0:T(8,128)S(1)} custom-call(bf16[128,2688]{1,0:T(8,128)(2,1)S(1)} %collective-permute-done.3.refs_0_.refs_3_.refs_4_, bf16[16,2560]{1,0:T(8,128)(2,1)S(1)} %pad_maximum_fusion.1.refs_1_, bf16[128,2688]{1,0:T(8,128)(2,1)S(1)} %pad_maximum_fusion.refs_2_, ...), custom_call_target="tpu_custom_call" | custom-call | flops 1342177280 | bytes 1966080 | tf_op jit(solution)/shard_map/pallas_call | solution.py:110
  31.2 1.9 %shard_map.49 = bf16[16,16,1024]{2,1,0:T(8,128)(2,1)S(1)} custom-call(bf16[128,2688]{1,0:T(8,128)(2,1)S(1)} %collective-permute-done.3.refs_0_.refs_3_.refs_4_, bf16[16,1536]{1,0:T(8,128)(2,1)S(1)} %pad_maximum_fusion.2.refs_1_, bf16[128,1536]{1,0:T(8,128)(2,1)S(1)} %maximum_select_fusion.1.refs_2_, ...), custom_call_target="tpu_custom_call" | custom-call | flops 805306368 | bytes 1179648 | tf_op jit(solution)/shard_map/pallas_call | solution.py:110
  33.0 2.3 %collective-permute-start.4 = (bf16[16,16,1024]{2,1,0:T(8,128)(2,1)S(1)}, bf16[16,16,1024]{2,1,0:T(8,128)(2,1)S(1)}, u32[]{:S(2)}, u32[]{:S(2)}) collective-permute-start(bf16[16,16,1024]{2,1,0:T(8,128)(2,1)S(1)} %shard_map.49), channel_id=1, source_target_pairs={{0,16},{16,0},{32,48},{48,32},{64,80},{80,64},{96,112},{112,96},{1... | collective-permute-start | bytes 1572872 | tf_op jit(solution)/shard_map/ppermute | solution.py:31
  35.3 1.9 %shard_map.48 = bf16[16,16,1024]{2,1,0:T(8,128)(2,1)S(1)} custom-call(bf16[128,2688]{1,0:T(8,128)(2,1)S(1)} %collective-permute-done.refs_4_.refs_0_.refs_3_, bf16[16,1536]{1,0:T(8,128)(2,1)S(1)} %pad_maximum_fusion.2.refs_1_, bf16[128,1536]{1,0:T(8,128)(2,1)S(1)} %maximum_select_fusion.1.refs_2_, ...), custom_call_target="tpu_custom_call" | custom-call | flops 805306368 | bytes 1179648 | tf_op jit(solution)/shard_map/pallas_call | solution.py:110
  37.2 0.2 add_convert_fusion
  37.4 18.7 %all_to_all.5 = bf16[16,16,1024]{2,1,0:T(8,128)(2,1)S(1)} all-to-all(bf16[16,16,1024]{2,1,0:T(8,128)(2,1)S(1)} %add_convert_fusion), channel_id=1, replica_groups={{0,32,64,96,128,160,192,224,256,288,320,352,384,416,448,480},{16,48,80,..., dimensions={0} | all-to-all | bytes 1048576 | tf_op jit(solution)/shard_map/all_to_all | solution.py:169
  56.2 1.9 %collective-permute-start.5 = (f32[16,1024]{1,0:T(8,128)S(1)}, f32[16,1024]{1,0:T(8,128)S(1)}, u32[]{:S(2)}, u32[]{:S(2)}) collective-permute-start(f32[16,1024]{1,0:T(8,128)S(1)} %convert_reduce_fusion), channel_id=1, source_target_pairs={{1,0},{2,1},{3,2},{4,3},{5,4},{6,5},{7,6},{8,7},{9,8},{10,9},{11,1... | collective-permute-start | bytes 196616 | tf_op jit(solution)/shard_map/ppermute | solution.py:27
  58.1 5.4 %collective-permute-done.5 = f32[16,1024]{1,0:T(8,128)S(1)} collective-permute-done((f32[16,1024]{1,0:T(8,128)S(1)}, f32[16,1024]{1,0:T(8,128)S(1)}, u32[]{:S(2)}, u32[]{:S(2)}) %collective-permute-start.5) | collective-permute-done | bytes 65568 | tf_op jit(solution)/shard_map/ppermute | solution.py:27
  63.6 1.9 %collective-permute-start.6 = (f32[2,4,1024]{2,1,0:T(4,128)S(1)}, f32[2,4,1024]{2,1,0:T(4,128)S(1)}, u32[]{:S(2)}, u32[]{:S(2)}) collective-permute-start(f32[2,4,1024]{2,1,0:T(4,128)S(1)} %fusion.10), channel_id=1, source_target_pairs={{0,16},{16,0},{32,48},{48,32},{64,80},{80,64},{96,112},{112,96},{1... | collective-permute-start | bytes 98312 | tf_op jit(solution)/shard_map/ppermute | solution.py:31
  65.6 1.2 %collective-permute-done.6 = f32[2,4,1024]{2,1,0:T(4,128)S(1)} collective-permute-done((f32[2,4,1024]{2,1,0:T(4,128)S(1)}, f32[2,4,1024]{2,1,0:T(4,128)S(1)}, u32[]{:S(2)}, u32[]{:S(2)}) %collective-permute-start.6) | collective-permute-done | bytes 32800 | tf_op jit(solution)/shard_map/ppermute | solution.py:31
  66.7 0.7 %maximum_multiply_fusion = f32[1,4,4,1024]{3,2,1,0:T(4,128)} fusion(f32[1,2,4,1024]{3,2,1,0:T(4,128)S(1)} %reverse_bitcast_fusion, f32[1,2,4,1024]{3,2,1,0:T(4,128)S(1)} %get-tuple-element.15, f32[4]{0:T(128)S(1)} %multiply_bitcast_fusion), kind=kLoop, calls=%fused_computation.19 | loop fusion | flops 32768 | bytes 131088 | tf_op jit(solution)/shard_map/mul | solution.py:179
  (23 shorter events, 0.3 us)
Async XLA Ops:
  0.0 1.8 %copy-start = (s32[1,64]{1,0:T(1,128)S(1)}, s32[1,64]{1,0:T(1,128)}, u32[]{:S(2)}) copy-start(s32[1,64]{1,0:T(1,128)} %param.5) | copy-start | bytes 772
  2.1 20.1 %collective-permute-start = (bf16[128,2688]{1,0:T(8,128)(2,1)S(1)}, bf16[128,2688]{1,0:T(8,128)(2,1)S(1)}, u32[]{:S(2)}, u32[]{:S(2)}) collective-permute-start(bf16[128,2688]{1,0:T(8,128)(2,1)S(1)} %pad_maximum_fusion.refs_2_), channel_id=1, source_target_pairs={{0,1},{1,2},{2,3},{3,4},{4,5},{5,6},{6,7},{7,8},{8,9},{9,10},{10,1... | collective-permute-start | bytes 2064392 | tf_op jit(solution)/shard_map/ppermute | solution.py:27
  7.2 19.6 %collective-permute-start.3 = (bf16[128,2688]{1,0:T(8,128)(2,1)S(1)}, bf16[128,2688]{1,0:T(8,128)(2,1)S(1)}, u32[]{:S(2)}, u32[]{:S(2)}) collective-permute-start(bf16[128,2688]{1,0:T(8,128)(2,1)S(1)} %pad_maximum_fusion.refs_2_), channel_id=1, source_target_pairs={{1,0},{2,1},{3,2},{4,3},{5,4},{6,5},{7,6},{8,7},{9,8},{10,9},{11,1... | collective-permute-start | bytes 2064392 | tf_op jit(solution)/shard_map/ppermute | solution.py:27
  10.3 20.8 %collective-permute-start.1 = (bf16[128,1536]{1,0:T(8,128)(2,1)S(1)}, bf16[128,1536]{1,0:T(8,128)(2,1)S(1)}, u32[]{:S(2)}, u32[]{:S(2)}) collective-permute-start(bf16[128,1536]{1,0:T(8,128)(2,1)S(1)} %maximum_select_fusion.1.refs_2_), channel_id=1, source_target_pairs={{0,1},{1,2},{2,3},{3,4},{4,5},{5,6},{6,7},{7,8},{8,9},{9,10},{10,1... | collective-permute-start | bytes 1179656 | tf_op jit(solution)/shard_map/ppermute | solution.py:27
  15.5 15.7 %collective-permute-start.2 = (bf16[128,1536]{1,0:T(8,128)(2,1)S(1)}, bf16[128,1536]{1,0:T(8,128)(2,1)S(1)}, u32[]{:S(2)}, u32[]{:S(2)}) collective-permute-start(bf16[128,1536]{1,0:T(8,128)(2,1)S(1)} %maximum_select_fusion.1.refs_2_), channel_id=1, source_target_pairs={{1,0},{2,1},{3,2},{4,3},{5,4},{6,5},{7,6},{8,7},{9,8},{10,9},{11,1... | collective-permute-start | bytes 1179656 | tf_op jit(solution)/shard_map/ppermute | solution.py:27
  33.0 4.2 %collective-permute-start.4 = (bf16[16,16,1024]{2,1,0:T(8,128)(2,1)S(1)}, bf16[16,16,1024]{2,1,0:T(8,128)(2,1)S(1)}, u32[]{:S(2)}, u32[]{:S(2)}) collective-permute-start(bf16[16,16,1024]{2,1,0:T(8,128)(2,1)S(1)} %shard_map.49), channel_id=1, source_target_pairs={{0,16},{16,0},{32,48},{48,32},{64,80},{80,64},{96,112},{112,96},{1... | collective-permute-start | bytes 1572872 | tf_op jit(solution)/shard_map/ppermute | solution.py:31
  37.4 28.1 %copy-start.1 = (s32[1,4]{1,0:T(1,128)S(1)}, s32[1,4]{1,0:T(1,128)}, u32[]{:S(2)}) copy-start(s32[1,4]{1,0:T(1,128)} %param.6) | copy-start | bytes 52
  56.2 7.4 %collective-permute-start.5 = (f32[16,1024]{1,0:T(8,128)S(1)}, f32[16,1024]{1,0:T(8,128)S(1)}, u32[]{:S(2)}, u32[]{:S(2)}) collective-permute-start(f32[16,1024]{1,0:T(8,128)S(1)} %convert_reduce_fusion), channel_id=1, source_target_pairs={{1,0},{2,1},{3,2},{4,3},{5,4},{6,5},{7,6},{8,7},{9,8},{10,9},{11,1... | collective-permute-start | bytes 196616 | tf_op jit(solution)/shard_map/ppermute | solution.py:27
  63.6 3.1 %collective-permute-start.6 = (f32[2,4,1024]{2,1,0:T(4,128)S(1)}, f32[2,4,1024]{2,1,0:T(4,128)S(1)}, u32[]{:S(2)}, u32[]{:S(2)}) collective-permute-start(f32[2,4,1024]{2,1,0:T(4,128)S(1)} %fusion.10), channel_id=1, source_target_pairs={{0,16},{16,0},{32,48},{48,32},{64,80},{80,64},{96,112},{112,96},{1... | collective-permute-start | bytes 98312 | tf_op jit(solution)/shard_map/ppermute | solution.py:31

commit v4 on v3

--- a/solution.py
+++ b/solution.py
@@ -10,7 +10,7 @@
 
 LAGS = 16
 CHUNKS = (5, 3)
-TILE = 512
+TILE = 256
 TAG = 128
 NT = (((1,), (1,)), ((), ()))
 TN = (((0,), (0,)), ((), ()))
@@ -47,8 +47,7 @@
     tag, table, own, near, far = refs[:5]
     before = None if first else refs[5]
     out = refs[5 if first else 6]
-    source_ref, kernel_ref, pair_ref = refs[-4:-1] if last else refs[-3:]
-    sums = refs[-1] if last else out
+    source_ref, kernel_ref, pair_ref = refs[-3:]
     channels, half = own.shape[0], table.shape[1] // 2
     source_count, lag_count = source_ref.shape[0], table.shape[0]
     per = TILE // lag_count
@@ -60,8 +59,7 @@
     pair_ref[:channels, :] = far[:, : 2 * half]
     pair_ref[channels:, :] = own[:, : 2 * half]
 
-    @pl.loop(0, source_count // per)
-    def _(step):
+    def build(step):
         for place in range(per):
             source = step * per + place
             rows = slice(place * lag_count, (place + 1) * lag_count)
@@ -69,27 +67,29 @@
             source_im = source_ref[pl.ds(source, 1), half:]
             upper = source_re * table_re + source_im * table_im
             lower = source_im * table_re - source_re * table_im
-            kernel_ref[rows, :half] = upper.astype(jnp.bfloat16)
-            kernel_ref[rows, half:] = lower.astype(jnp.bfloat16)
-        rows = pl.ds(pl.multiple_of(step * TILE, TILE), TILE)
+            kernel_ref[step % 2, rows, :half] = upper.astype(jnp.bfloat16)
+            kernel_ref[step % 2, rows, half:] = lower.astype(jnp.bfloat16)
+
+    def multiply(step):
+        rows = slice(step * TILE, (step + 1) * TILE)
         term = lax.dot_general(
-            kernel_ref[...], pair_ref[...], NT, preferred_element_type=jnp.float32
+            kernel_ref[step % 2], pair_ref[...], NT, preferred_element_type=jnp.float32
         )
         if not first:
             term = term + before[rows, :]
-        sums[rows, :] = term.astype(sums.dtype)
+        if last:
+            chips, each = out.shape[0], out.shape[1] // 2
+            turned = term.T.reshape(2, chips, each, TILE)
+            out[:, :, rows] = jnp.concatenate([turned[0], turned[1]], axis=1).astype(jnp.bfloat16)
+        else:
+            out[rows, :] = term
 
-    if last:
-        chips, rows = out.shape[0], out.shape[1] // 2
-        size = 2 * channels
-        to = lax.broadcasted_iota(jnp.int32, (size, size), 0)
-        frm = lax.broadcasted_iota(jnp.int32, (size, size), 1)
-        wanted = to // rows % 2 * channels + to // (2 * rows) * rows + to % rows
-        order = (frm == wanted).astype(jnp.float32).astype(jnp.bfloat16)
-        for start in range(0, source_count * lag_count, 256):
-            part = slice(start, start + 256)
-            turned = lax.dot_general(order, sums[part, :], NT, preferred_element_type=jnp.float32)
-            out[:, :, part] = turned.reshape(chips, 2 * rows, 256).astype(jnp.bfloat16)
+    steps = source_count // per
+    build(0)
+    for step in range(1, steps):
+        build(step)
+        multiply(step - 1)
+    multiply(steps - 1)
 
 
 def products(tag, source_count, table, own, near, far, before, last, chips):
@@ -98,11 +98,10 @@
     first = before is None
     scratch = [
         pltpu.VMEM((source_count, width), jnp.float32),
-        pltpu.VMEM((TILE, width), jnp.bfloat16),
+        pltpu.VMEM((2, TILE, width), jnp.bfloat16),
         pltpu.VMEM((2 * channels, width), jnp.bfloat16),
     ]
     if last:
-        scratch.append(pltpu.VMEM((columns, 2 * channels), jnp.bfloat16))
         shape = jax.ShapeDtypeStruct((chips, 2 * channels // chips, columns), jnp.bfloat16)
     else:
         shape = jax.ShapeDtypeStruct((columns, 2 * channels), jnp.float32)
@@ -134,9 +133,10 @@
         re, im = array[..., :bin_count], array[..., bin_count:]
         return jnp.concatenate([re[..., bins], im[..., bins]], axis=-1)
 
-    chosen = jnp.pad(source_channels[0], (0, TAG - source_channels.shape[1]), constant_values=channels)
-    channel_ids = lax.broadcasted_iota(jnp.int32, (channels, TAG), 0)
-    hot = jnp.logical_and(chosen[None, :] == channel_ids, live_rows).astype(jnp.bfloat16)
+    sources = source_channels.shape[1]
+    channel_ids = lax.broadcasted_iota(jnp.int32, (channels, sources), 0)
+    hot = jnp.logical_and(source_channels == channel_ids, live_rows).astype(jnp.bfloat16)
+    hot = jnp.concatenate([hot, jnp.zeros((channels, TAG - sources), jnp.bfloat16)], axis=1)
     own, one, other = [], [], []
     for index in range(len(parts)):
         piece = chunk_of(block, index)
@@ -149,8 +149,6 @@
         block, _ = lax.optimization_barrier((block, piece))
     table = make_table(bin_count, LAGS)
     table = jnp.concatenate([table[0], table[1]], axis=-1)
-    sources = source_channels.shape[1]
-
     def side(near, far, sums, index):
         last = index == len(parts) - 1
         return products(

time: 68.1 us -> 67.9 us (level)
  Pallas kernels: 8.04 us -> 7 us
    pallas_call x4, Pallas kernels: 8.04 us -> 7 us  [products(): pl.pallas_call(functools.partial(products_kernel, first, last), out_shape...]
  transfers between devices with their start and end apart: 7 -> 7, of which waited for: 4 -> 5; matrix products, arithmetic and copies ran while one was open for 3% -> 3% of each run, Pallas kernels for 9% -> 8%
where the time goes in v4:
time: 67.9 us; the launch traced here: 67.3 us
  starting transfers between devices  20.3 us (30%)
  blocking collectives  18.9 us (28%)
  waiting for transfers between devices  15.7 us (23%)
  Pallas kernels  7 us (10%)
  local copies, waits for them, and re-layouts  2.52 us (4%)
  other arithmetic  2.04 us (3%)
  between operations  0.92 us (1%)
    all_to_all x1, blocking collectives, local(): lax.all_to_all(both, 'seg', 0, 0, axis_index_groups=groups, tiled=True)  18.9 us
    ppermute x5, starting transfers between devices, passed_along(): return lax.ppermute(value, ('seg', 'blk'), pairs)  15.9 us
    ppermute x5, waiting for transfers between devices, passed_along(): return lax.ppermute(value, ('seg', 'blk'), pairs)  14.5 us
    pallas_call x4, Pallas kernels, products(): pl.pallas_call(functools.partial(products_kernel, first, last), out_shape...  7 us
    ppermute x2, starting transfers between devices, to_other_core(): lax.ppermute(value, 'seg', [(i, i ^ 1) for i in range(lax.axis_size('seg'...  4.34 us
    slice x6, local copies, waits for them, and re-layouts, chunk_of(): return jnp.concatenate([re[..., bins], im[..., bins]], axis=-1)  2.2 us
  transfers between devices with their start and end apart: 7, of which 5 were waited for; matrix products, arithmetic and copies ran while one was open for 3% of the time, Pallas kernels for 8%

profile of v4, /device:TPU:96, one launch (start us, length us, event | category | flops | bytes accessed | tf_op | source)
XLA Modules:
  0.0 67.3 jit_solution(10063979053460793036)
XLA Ops:
  0.0 1.1 %fusion.13 = (bf16[128,1280]{1,0:T(8,128)(2,1)S(1)}, bf16[128,1280]{1,0:T(8,128)(2,1)S(1)}) fusion(bf16[128,4096]{1,0:T(8,128)(2,1)} %bitcast.35), kind=kLoop, calls=%fused_computation.34 | loop fusion | bytes 1310720 | tf_op jit(solution)/shard_map/slice | solution.py:134
  1.9 0.2 maximum_select_fusion
  2.1 0.3 concatenate.32.refs_2_
  2.4 5.0 %collective-permute-start = (bf16[128,2688]{1,0:T(8,128)(2,1)S(1)}, bf16[128,2688]{1,0:T(8,128)(2,1)S(1)}, u32[]{:S(2)}, u32[]{:S(2)}) collective-permute-start(bf16[128,2688]{1,0:T(8,128)(2,1)S(1)} %concatenate.32.refs_2_), channel_id=1, source_target_pairs={{0,1},{1,2},{2,3},{3,4},{4,5},{5,6},{6,7},{7,8},{8,9},{9,10},{10,1... | collective-permute-start | bytes 2064392 | tf_op jit(solution)/shard_map/ppermute | solution.py:27
  7.4 1.9 %collective-permute-start.3 = (bf16[128,2688]{1,0:T(8,128)(2,1)S(1)}, bf16[128,2688]{1,0:T(8,128)(2,1)S(1)}, u32[]{:S(2)}, u32[]{:S(2)}) collective-permute-start(bf16[128,2688]{1,0:T(8,128)(2,1)S(1)} %concatenate.32.refs_2_), channel_id=1, source_target_pairs={{1,0},{2,1},{3,2},{4,3},{5,4},{6,5},{7,6},{8,7},{9,8},{10,9},{11,1... | collective-permute-start | bytes 2064392 | tf_op jit(solution)/shard_map/ppermute | solution.py:27
  9.3 1.1 %fusion.12 = (bf16[128,768]{1,0:T(8,128)(2,1)S(1)}, bf16[128,768]{1,0:T(8,128)(2,1)S(1)}) fusion(bf16[128,4096]{1,0:T(8,128)(2,1)} %bitcast.36), kind=kLoop, calls=%fused_computation.33 | loop fusion | bytes 786432 | tf_op jit(solution)/shard_map/slice | solution.py:134
  10.5 5.1 %collective-permute-start.1 = (bf16[128,1536]{1,0:T(8,128)(2,1)S(1)}, bf16[128,1536]{1,0:T(8,128)(2,1)S(1)}, u32[]{:S(2)}, u32[]{:S(2)}) collective-permute-start(bf16[128,1536]{1,0:T(8,128)(2,1)S(1)} %maximum_select_fusion.1.refs_2_), channel_id=1, source_target_pairs={{0,1},{1,2},{2,3},{3,4},{4,5},{5,6},{6,7},{7,8},{8,9},{9,10},{10,1... | collective-permute-start | bytes 1179656 | tf_op jit(solution)/shard_map/ppermute | solution.py:27
  15.7 1.9 %collective-permute-start.2 = (bf16[128,1536]{1,0:T(8,128)(2,1)S(1)}, bf16[128,1536]{1,0:T(8,128)(2,1)S(1)}, u32[]{:S(2)}, u32[]{:S(2)}) collective-permute-start(bf16[128,1536]{1,0:T(8,128)(2,1)S(1)} %maximum_select_fusion.1.refs_2_), channel_id=1, source_target_pairs={{1,0},{2,1},{3,2},{4,3},{5,4},{6,5},{7,6},{8,7},{9,8},{10,9},{11,1... | collective-permute-start | bytes 1179656 | tf_op jit(solution)/shard_map/ppermute | solution.py:27
  17.6 0.6 fusion.6
  18.3 4.2 %collective-permute-done.refs_4_.refs_0_.refs_3_ = bf16[128,2688]{1,0:T(8,128)(2,1)S(1)} collective-permute-done((bf16[128,2688]{1,0:T(8,128)(2,1)S(1)}, bf16[128,2688]{1,0:T(8,128)(2,1)S(1)}, u32[]{:S(2)}, u32[]{:S(2)}) %collective-permute-start) | collective-permute-done | bytes 688160 | tf_op jit(solution)/shard_map/ppermute | solution.py:27
  22.5 4.6 %collective-permute-done.3.refs_0_.refs_3_.refs_4_ = bf16[128,2688]{1,0:T(8,128)(2,1)S(1)} collective-permute-done((bf16[128,2688]{1,0:T(8,128)(2,1)S(1)}, bf16[128,2688]{1,0:T(8,128)(2,1)S(1)}, u32[]{:S(2)}, u32[]{:S(2)}) %collective-permute-start.3) | collective-permute-done | bytes 688160 | tf_op jit(solution)/shard_map/ppermute | solution.py:27
  27.1 2.0 %shard_map.47.refs_5_ = f32[1024,256]{1,0:T(8,128)S(1)} custom-call(bf16[128,2688]{1,0:T(8,128)(2,1)S(1)} %collective-permute-done.refs_4_.refs_0_.refs_3_, bf16[16,2560]{1,0:T(8,128)(2,1)S(1)} %pad_maximum_fusion.refs_1_, bf16[128,2688]{1,0:T(8,128)(2,1)S(1)} %concatenate.32.refs_2_, bf16[128,2688]{1,0:T(8,128)(2,1)S(1)} %collective-permute-done.refs_4_.refs_0_.refs_3_, ...), custom_call_target="tpu_custom_call" | custom-call | flops 1342177280 | bytes 1966080 | tf_op jit(solution)/shard_map/pallas_call | solution.py:109
  29.1 2.0 %shard_map.46.refs_5_ = f32[1024,256]{1,0:T(8,128)S(1)} custom-call(bf16[128,2688]{1,0:T(8,128)(2,1)S(1)} %collective-permute-done.3.refs_0_.refs_3_.refs_4_, bf16[16,2560]{1,0:T(8,128)(2,1)S(1)} %pad_maximum_fusion.refs_1_, bf16[128,2688]{1,0:T(8,128)(2,1)S(1)} %concatenate.32.refs_2_, bf16[128,2688]{1,0:T(8,128)(2,1)S(1)} %collective-permute-done.3.refs_0_.refs_3_.refs_4_, ...), custom_call_target="tpu_custom_call" | custom-call | flops 1342177280 | bytes 1966080 | tf_op jit(solution)/shard_map/pallas_call | solution.py:109
  31.1 0.1 collective-permute-done.2.refs_4_.refs_3_
  31.3 1.5 %shard_map.49 = bf16[16,16,1024]{2,1,0:T(8,128)(2,1)S(1)} custom-call(bf16[128,2688]{1,0:T(8,128)(2,1)S(1)} %collective-permute-done.3.refs_0_.refs_3_.refs_4_, bf16[16,1536]{1,0:T(8,128)(2,1)S(1)} %pad_maximum_fusion.1.refs_1_, bf16[128,1536]{1,0:T(8,128)(2,1)S(1)} %maximum_select_fusion.1.refs_2_, ...), custom_call_target="tpu_custom_call" | custom-call | flops 805306368 | bytes 1179648 | tf_op jit(solution)/shard_map/pallas_call | solution.py:109
  32.7 2.4 %collective-permute-start.4 = (bf16[16,16,1024]{2,1,0:T(8,128)(2,1)S(1)}, bf16[16,16,1024]{2,1,0:T(8,128)(2,1)S(1)}, u32[]{:S(2)}, u32[]{:S(2)}) collective-permute-start(bf16[16,16,1024]{2,1,0:T(8,128)(2,1)S(1)} %shard_map.49), channel_id=1, source_target_pairs={{0,16},{16,0},{32,48},{48,32},{64,80},{80,64},{96,112},{112,96},{1... | collective-permute-start | bytes 1572872 | tf_op jit(solution)/shard_map/ppermute | solution.py:31
  35.2 1.5 %shard_map.48 = bf16[16,16,1024]{2,1,0:T(8,128)(2,1)S(1)} custom-call(bf16[128,2688]{1,0:T(8,128)(2,1)S(1)} %collective-permute-done.refs_4_.refs_0_.refs_3_, bf16[16,1536]{1,0:T(8,128)(2,1)S(1)} %pad_maximum_fusion.1.refs_1_, bf16[128,1536]{1,0:T(8,128)(2,1)S(1)} %maximum_select_fusion.1.refs_2_, ...), custom_call_target="tpu_custom_call" | custom-call | flops 805306368 | bytes 1179648 | tf_op jit(solution)/shard_map/pallas_call | solution.py:109
  36.7 0.2 add_convert_fusion
  36.9 18.9 %all_to_all.5 = bf16[16,16,1024]{2,1,0:T(8,128)(2,1)S(1)} all-to-all(bf16[16,16,1024]{2,1,0:T(8,128)(2,1)S(1)} %add_convert_fusion), channel_id=1, replica_groups={{0,32,64,96,128,160,192,224,256,288,320,352,384,416,448,480},{16,48,80,..., dimensions={0} | all-to-all | bytes 1048576 | tf_op jit(solution)/shard_map/all_to_all | solution.py:167
  55.8 1.9 %collective-permute-start.5 = (f32[16,1024]{1,0:T(8,128)S(1)}, f32[16,1024]{1,0:T(8,128)S(1)}, u32[]{:S(2)}, u32[]{:S(2)}) collective-permute-start(f32[16,1024]{1,0:T(8,128)S(1)} %convert_reduce_fusion), channel_id=1, source_target_pairs={{1,0},{2,1},{3,2},{4,3},{5,4},{6,5},{7,6},{8,7},{9,8},{10,9},{11,1... | collective-permute-start | bytes 196616 | tf_op jit(solution)/shard_map/ppermute | solution.py:27
  57.8 5.6 %collective-permute-done.5 = f32[16,1024]{1,0:T(8,128)S(1)} collective-permute-done((f32[16,1024]{1,0:T(8,128)S(1)}, f32[16,1024]{1,0:T(8,128)S(1)}, u32[]{:S(2)}, u32[]{:S(2)}) %collective-permute-start.5) | collective-permute-done | bytes 65568 | tf_op jit(solution)/shard_map/ppermute | solution.py:27
  63.4 1.9 %collective-permute-start.6 = (f32[2,4,1024]{2,1,0:T(4,128)S(1)}, f32[2,4,1024]{2,1,0:T(4,128)S(1)}, u32[]{:S(2)}, u32[]{:S(2)}) collective-permute-start(f32[2,4,1024]{2,1,0:T(4,128)S(1)} %fusion.10), channel_id=1, source_target_pairs={{0,16},{16,0},{32,48},{48,32},{64,80},{80,64},{96,112},{112,96},{1... | collective-permute-start | bytes 98312 | tf_op jit(solution)/shard_map/ppermute | solution.py:31
  65.4 1.2 %collective-permute-done.6 = f32[2,4,1024]{2,1,0:T(4,128)S(1)} collective-permute-done((f32[2,4,1024]{2,1,0:T(4,128)S(1)}, f32[2,4,1024]{2,1,0:T(4,128)S(1)}, u32[]{:S(2)}, u32[]{:S(2)}) %collective-permute-start.6) | collective-permute-done | bytes 32800 | tf_op jit(solution)/shard_map/ppermute | solution.py:31
  66.6 0.7 %maximum_multiply_fusion = f32[1,4,4,1024]{3,2,1,0:T(4,128)} fusion(f32[1,2,4,1024]{3,2,1,0:T(4,128)S(1)} %reverse_bitcast_fusion, f32[1,2,4,1024]{3,2,1,0:T(4,128)S(1)} %get-tuple-element.15, f32[4]{0:T(128)S(1)} %multiply_bitcast_fusion), kind=kLoop, calls=%fused_computation.18 | loop fusion | flops 32768 | bytes 131088 | tf_op jit(solution)/shard_map/mul | solution.py:177
  (23 shorter events, 0.4 us)
Async XLA Ops:
  0.0 1.8 %copy-start = (s32[1,64]{1,0:T(1,128)S(1)}, s32[1,64]{1,0:T(1,128)}, u32[]{:S(2)}) copy-start(s32[1,64]{1,0:T(1,128)} %param.5) | copy-start | bytes 772
  2.4 20.1 %collective-permute-start = (bf16[128,2688]{1,0:T(8,128)(2,1)S(1)}, bf16[128,2688]{1,0:T(8,128)(2,1)S(1)}, u32[]{:S(2)}, u32[]{:S(2)}) collective-permute-start(bf16[128,2688]{1,0:T(8,128)(2,1)S(1)} %concatenate.32.refs_2_), channel_id=1, source_target_pairs={{0,1},{1,2},{2,3},{3,4},{4,5},{5,6},{6,7},{7,8},{8,9},{9,10},{10,1... | collective-permute-start | bytes 2064392 | tf_op jit(solution)/shard_map/ppermute | solution.py:27
  7.4 19.6 %collective-permute-start.3 = (bf16[128,2688]{1,0:T(8,128)(2,1)S(1)}, bf16[128,2688]{1,0:T(8,128)(2,1)S(1)}, u32[]{:S(2)}, u32[]{:S(2)}) collective-permute-start(bf16[128,2688]{1,0:T(8,128)(2,1)S(1)} %concatenate.32.refs_2_), channel_id=1, source_target_pairs={{1,0},{2,1},{3,2},{4,3},{5,4},{6,5},{7,6},{8,7},{9,8},{10,9},{11,1... | collective-permute-start | bytes 2064392 | tf_op jit(solution)/shard_map/ppermute | solution.py:27
  10.5 20.6 %collective-permute-start.1 = (bf16[128,1536]{1,0:T(8,128)(2,1)S(1)}, bf16[128,1536]{1,0:T(8,128)(2,1)S(1)}, u32[]{:S(2)}, u32[]{:S(2)}) collective-permute-start(bf16[128,1536]{1,0:T(8,128)(2,1)S(1)} %maximum_select_fusion.1.refs_2_), channel_id=1, source_target_pairs={{0,1},{1,2},{2,3},{3,4},{4,5},{5,6},{6,7},{7,8},{8,9},{9,10},{10,1... | collective-permute-start | bytes 1179656 | tf_op jit(solution)/shard_map/ppermute | solution.py:27
  15.7 15.6 %collective-permute-start.2 = (bf16[128,1536]{1,0:T(8,128)(2,1)S(1)}, bf16[128,1536]{1,0:T(8,128)(2,1)S(1)}, u32[]{:S(2)}, u32[]{:S(2)}) collective-permute-start(bf16[128,1536]{1,0:T(8,128)(2,1)S(1)} %maximum_select_fusion.1.refs_2_), channel_id=1, source_target_pairs={{1,0},{2,1},{3,2},{4,3},{5,4},{6,5},{7,6},{8,7},{9,8},{10,9},{11,1... | collective-permute-start | bytes 1179656 | tf_op jit(solution)/shard_map/ppermute | solution.py:27
  32.7 3.9 %collective-permute-start.4 = (bf16[16,16,1024]{2,1,0:T(8,128)(2,1)S(1)}, bf16[16,16,1024]{2,1,0:T(8,128)(2,1)S(1)}, u32[]{:S(2)}, u32[]{:S(2)}) collective-permute-start(bf16[16,16,1024]{2,1,0:T(8,128)(2,1)S(1)} %shard_map.49), channel_id=1, source_target_pairs={{0,16},{16,0},{32,48},{48,32},{64,80},{80,64},{96,112},{112,96},{1... | collective-permute-start | bytes 1572872 | tf_op jit(solution)/shard_map/ppermute | solution.py:31
  36.9 28.5 %copy-start.1 = (s32[1,4]{1,0:T(1,128)S(1)}, s32[1,4]{1,0:T(1,128)}, u32[]{:S(2)}) copy-start(s32[1,4]{1,0:T(1,128)} %param.6) | copy-start | bytes 52
  55.8 7.5 %collective-permute-start.5 = (f32[16,1024]{1,0:T(8,128)S(1)}, f32[16,1024]{1,0:T(8,128)S(1)}, u32[]{:S(2)}, u32[]{:S(2)}) collective-permute-start(f32[16,1024]{1,0:T(8,128)S(1)} %convert_reduce_fusion), channel_id=1, source_target_pairs={{1,0},{2,1},{3,2},{4,3},{5,4},{6,5},{7,6},{8,7},{9,8},{10,9},{11,1... | collective-permute-start | bytes 196616 | tf_op jit(solution)/shard_map/ppermute | solution.py:27
  63.4 3.1 %collective-permute-start.6 = (f32[2,4,1024]{2,1,0:T(4,128)S(1)}, f32[2,4,1024]{2,1,0:T(4,128)S(1)}, u32[]{:S(2)}, u32[]{:S(2)}) collective-permute-start(f32[2,4,1024]{2,1,0:T(4,128)S(1)} %fusion.10), channel_id=1, source_target_pairs={{0,16},{16,0},{32,48},{48,32},{64,80},{80,64},{96,112},{112,96},{1... | collective-permute-start | bytes 98312 | tf_op jit(solution)/shard_map/ppermute | solution.py:31

commit v5 on v4

--- a/solution.py
+++ b/solution.py
@@ -90,6 +90,34 @@
         build(step)
         multiply(step - 1)
     multiply(steps - 1)
+
+
+def pack_kernel(count, chosen_ref, block_ref, *refs):
+    *outs, chosen, block, chosen_sem, block_sem = refs
+    copies = (
+        pltpu.make_async_copy(block_ref, block, block_sem),
+        pltpu.make_async_copy(chosen_ref, chosen, chosen_sem),
+    )
+    for copy in copies:
+        copy.start()
+    for copy in copies:
+        copy.wait()
+    channels, bin_count = block.shape[0], block.shape[1] // 2
+    start = 0
+    for index, out in enumerate(outs):
+        bins = (out.shape[1] - (TAG if index == 0 else 0)) // 2
+        live = lax.broadcasted_iota(jnp.int32, (channels, bins), 0) < count[0]
+        for half in range(2):
+            part = block[:, half * bin_count + start : half * bin_count + start + bins]
+            part = jnp.where(live, part.astype(jnp.float32), 0.0).astype(jnp.bfloat16)
+            out[:, half * bins : (half + 1) * bins] = part
+        start += bins
+    tag = outs[0].shape[1] - TAG
+    sources = chosen.shape[1]
+    rows = lax.broadcasted_iota(jnp.int32, (channels, sources), 0)
+    hot = jnp.logical_and(chosen[...] == rows, rows < count[0])
+    outs[0][:, tag:] = jnp.zeros((channels, TAG), jnp.bfloat16)
+    outs[0][:, tag : tag + sources] = jnp.where(hot, 1.0, 0.0).astype(jnp.bfloat16)
 
 
 def products(tag, source_count, table, own, near, far, before, last, chips):
@@ -124,7 +152,6 @@
     channels, bin_count = block.shape[0], block.shape[1] // 2
     segments = lax.axis_size("seg")
     chips, rows = segments // 2, channels // segments
-    live_rows = lax.broadcasted_iota(jnp.int32, (channels, 1), 0) < channel_counts[0]
     parts = [bin_count * share // sum(CHUNKS) for share in CHUNKS]
     starts = [sum(parts[:index]) for index in range(len(parts))]
 
@@ -134,19 +161,23 @@
         return jnp.concatenate([re[..., bins], im[..., bins]], axis=-1)
 
     sources = source_channels.shape[1]
-    channel_ids = lax.broadcasted_iota(jnp.int32, (channels, sources), 0)
-    hot = jnp.logical_and(source_channels == channel_ids, live_rows).astype(jnp.bfloat16)
-    hot = jnp.concatenate([hot, jnp.zeros((channels, TAG - sources), jnp.bfloat16)], axis=1)
-    own, one, other = [], [], []
-    for index in range(len(parts)):
-        piece = chunk_of(block, index)
-        piece = jnp.where(live_rows, piece, jnp.zeros_like(piece))
-        if index == 0:
-            piece = jnp.concatenate([piece, hot], axis=1)
-        own.append(piece)
-        one.append(passed_along(piece, 1))
-        other.append(passed_along(piece, -1))
-        block, _ = lax.optimization_barrier((block, piece))
+    vmem = pl.BlockSpec(memory_space=pltpu.VMEM)
+    own = pl.pallas_call(
+        pack_kernel,
+        out_shape=[
+            jax.ShapeDtypeStruct((channels, 2 * bins + (0 if index else TAG)), jnp.bfloat16)
+            for index, bins in enumerate(parts)
+        ],
+        in_specs=[pl.BlockSpec(memory_space=pltpu.SMEM)] + [pl.BlockSpec(memory_space=pltpu.HBM)] * 2,
+        out_specs=[vmem] * len(parts),
+        scratch_shapes=[
+            pltpu.VMEM(source_channels.shape, jnp.int32), pltpu.VMEM(block.shape, jnp.bfloat16),
+            pltpu.SemaphoreType.DMA(()), pltpu.SemaphoreType.DMA(()),
+        ],
+        compiler_params=pltpu.CompilerParams(vmem_limit_bytes=16 << 20),
+    )(channel_counts, source_channels, block)
+    one = [passed_along(piece, 1) for piece in own]
+    other = [passed_along(piece, -1) for piece in own]
     table = make_table(bin_count, LAGS)
     table = jnp.concatenate([table[0], table[1]], axis=-1)
     def side(near, far, sums, index):

time: 67.9 us -> 68.4 us (level)
  waiting for transfers between devices: 15.7 us -> 16.9 us
    slice x6 -> x4, local copies, waits for them, and re-layouts: 2.2 us -> 0.02 us  [chunk_of(): return jnp.concatenate([re[..., bins], im[..., bins]], axis=-1)]
    unnamed x4 -> x6, local copies, waits for them, and re-layouts: 0.01 us -> 1.88 us
    ppermute x5, waiting for transfers between devices: 14.5 us -> 15.7 us  [passed_along(): return lax.ppermute(value, ('seg', 'blk'), pairs)]
  transfers between devices with their start and end apart: 7 -> 7, of which waited for: 5 -> 5; matrix products, arithmetic and copies ran while one was open for 3% -> 1% of each run, Pallas kernels for 8% -> 8%
where the time goes in v5:
time: 68.4 us; the launch traced here: 67.7 us
  starting transfers between devices  20.3 us (30%)
  blocking collectives  18.9 us (28%)
  waiting for transfers between devices  16.9 us (25%)
  Pallas kernels  7.28 us (11%)
  local copies, waits for them, and re-layouts  1.92 us (3%)
  other arithmetic  1.63 us (2%)
  between operations  0.89 us (1%)
    all_to_all x1, blocking collectives, local(): lax.all_to_all(both, 'seg', 0, 0, axis_index_groups=groups, tiled=True)  18.9 us
    ppermute x5, starting transfers between devices, passed_along(): return lax.ppermute(value, ('seg', 'blk'), pairs)  15.9 us
    ppermute x5, waiting for transfers between devices, passed_along(): return lax.ppermute(value, ('seg', 'blk'), pairs)  15.7 us
    pallas_call x4, Pallas kernels, products(): pl.pallas_call(functools.partial(products_kernel, first, last), out_shape...  7 us
    ppermute x2, starting transfers between devices, to_other_core(): lax.ppermute(value, 'seg', [(i, i ^ 1) for i in range(lax.axis_size('seg'...  4.34 us
    unnamed x6, local copies, waits for them, and re-layouts  1.88 us
  transfers between devices with their start and end apart: 7, of which 5 were waited for; matrix products, arithmetic and copies ran while one was open for 1% of the time, Pallas kernels for 8%

profile of v5, /device:TPU:96, one launch (start us, length us, event | category | flops | bytes accessed | tf_op | source)
XLA Modules:
  0.0 67.7 jit_solution(16368462760738553663)
XLA Ops:
  0.7 0.6 copy-done.1
  1.3 1.2 %copy-done = bf16[1,1,128,4096]{3,2,1,0:T(8,128)(2,1)S(1)} copy-done((bf16[1,1,128,4096]{3,2,1,0:T(8,128)(2,1)S(1)}, bf16[1,1,128,4096]{3,2,1,0:T(8,128)(2,1)}, u32[]{:S(2)}) %copy-start) | copy-done | bytes 1048600
  2.5 0.3 shard_map.46
  2.8 5.0 %collective-permute-start = (bf16[128,2688]{1,0:T(8,128)(2,1)S(1)}, bf16[128,2688]{1,0:T(8,128)(2,1)S(1)}, u32[]{:S(2)}, u32[]{:S(2)}) collective-permute-start(bf16[128,2688]{1,0:T(8,128)(2,1)S(1)} %get-tuple-element.9.refs_2_), channel_id=1, source_target_pairs={{0,1},{1,2},{2,3},{3,4},{4,5},{5,6},{6,7},{7,8},{8,9},{9,10},{10,1... | collective-permute-start | bytes 2064392 | tf_op jit(solution)/shard_map/ppermute | solution.py:27
  7.9 1.9 %collective-permute-start.3 = (bf16[128,2688]{1,0:T(8,128)(2,1)S(1)}, bf16[128,2688]{1,0:T(8,128)(2,1)S(1)}, u32[]{:S(2)}, u32[]{:S(2)}) collective-permute-start(bf16[128,2688]{1,0:T(8,128)(2,1)S(1)} %get-tuple-element.9.refs_2_), channel_id=1, source_target_pairs={{1,0},{2,1},{3,2},{4,3},{5,4},{6,5},{7,6},{8,7},{9,8},{10,9},{11,1... | collective-permute-start | bytes 2064392 | tf_op jit(solution)/shard_map/ppermute | solution.py:27
  9.8 5.1 %collective-permute-start.1 = (bf16[128,1536]{1,0:T(8,128)(2,1)S(1)}, bf16[128,1536]{1,0:T(8,128)(2,1)S(1)}, u32[]{:S(2)}, u32[]{:S(2)}) collective-permute-start(bf16[128,1536]{1,0:T(8,128)(2,1)S(1)} %get-tuple-element.10.refs_2_), channel_id=1, source_target_pairs={{0,1},{1,2},{2,3},{3,4},{4,5},{5,6},{6,7},{7,8},{8,9},{9,10},{10,1... | collective-permute-start | bytes 1179656 | tf_op jit(solution)/shard_map/ppermute | solution.py:27
  14.9 1.9 %collective-permute-start.2 = (bf16[128,1536]{1,0:T(8,128)(2,1)S(1)}, bf16[128,1536]{1,0:T(8,128)(2,1)S(1)}, u32[]{:S(2)}, u32[]{:S(2)}) collective-permute-start(bf16[128,1536]{1,0:T(8,128)(2,1)S(1)} %get-tuple-element.10.refs_2_), channel_id=1, source_target_pairs={{1,0},{2,1},{3,2},{4,3},{5,4},{6,5},{7,6},{8,7},{9,8},{10,9},{11,1... | collective-permute-start | bytes 1179656 | tf_op jit(solution)/shard_map/ppermute | solution.py:27
  16.9 0.6 fusion.6
  17.6 5.4 %collective-permute-done.refs_4_.refs_0_.refs_3_ = bf16[128,2688]{1,0:T(8,128)(2,1)S(1)} collective-permute-done((bf16[128,2688]{1,0:T(8,128)(2,1)S(1)}, bf16[128,2688]{1,0:T(8,128)(2,1)S(1)}, u32[]{:S(2)}, u32[]{:S(2)}) %collective-permute-start) | collective-permute-done | bytes 688160 | tf_op jit(solution)/shard_map/ppermute | solution.py:27
  22.9 4.6 %collective-permute-done.3.refs_0_.refs_3_.refs_4_ = bf16[128,2688]{1,0:T(8,128)(2,1)S(1)} collective-permute-done((bf16[128,2688]{1,0:T(8,128)(2,1)S(1)}, bf16[128,2688]{1,0:T(8,128)(2,1)S(1)}, u32[]{:S(2)}, u32[]{:S(2)}) %collective-permute-start.3) | collective-permute-done | bytes 688160 | tf_op jit(solution)/shard_map/ppermute | solution.py:27
  27.5 2.0 %shard_map.48.refs_5_ = f32[1024,256]{1,0:T(8,128)S(1)} custom-call(bf16[128,2688]{1,0:T(8,128)(2,1)S(1)} %collective-permute-done.refs_4_.refs_0_.refs_3_, bf16[16,2560]{1,0:T(8,128)(2,1)S(1)} %pad_maximum_fusion.refs_1_, bf16[128,2688]{1,0:T(8,128)(2,1)S(1)} %get-tuple-element.9.refs_2_, ...), custom_call_target="tpu_custom_call" | custom-call | flops 1342177280 | bytes 1966080 | tf_op jit(solution)/shard_map/pallas_call | solution.py:137
  29.5 2.0 %shard_map.47.refs_5_ = f32[1024,256]{1,0:T(8,128)S(1)} custom-call(bf16[128,2688]{1,0:T(8,128)(2,1)S(1)} %collective-permute-done.3.refs_0_.refs_3_.refs_4_, bf16[16,2560]{1,0:T(8,128)(2,1)S(1)} %pad_maximum_fusion.refs_1_, bf16[128,2688]{1,0:T(8,128)(2,1)S(1)} %get-tuple-element.9.refs_2_, ...), custom_call_target="tpu_custom_call" | custom-call | flops 1342177280 | bytes 1966080 | tf_op jit(solution)/shard_map/pallas_call | solution.py:137
  31.6 0.1 collective-permute-done.2.refs_4_.refs_3_
  31.7 1.5 %shard_map.50 = bf16[16,16,1024]{2,1,0:T(8,128)(2,1)S(1)} custom-call(bf16[128,2688]{1,0:T(8,128)(2,1)S(1)} %collective-permute-done.3.refs_0_.refs_3_.refs_4_, bf16[16,1536]{1,0:T(8,128)(2,1)S(1)} %pad_maximum_fusion.1.refs_1_, bf16[128,1536]{1,0:T(8,128)(2,1)S(1)} %get-tuple-element.10.refs_2_, ...), custom_call_target="tpu_custom_call" | custom-call | flops 805306368 | bytes 1179648 | tf_op jit(solution)/shard_map/pallas_call | solution.py:137
  33.2 2.4 %collective-permute-start.4 = (bf16[16,16,1024]{2,1,0:T(8,128)(2,1)S(1)}, bf16[16,16,1024]{2,1,0:T(8,128)(2,1)S(1)}, u32[]{:S(2)}, u32[]{:S(2)}) collective-permute-start(bf16[16,16,1024]{2,1,0:T(8,128)(2,1)S(1)} %shard_map.50), channel_id=1, source_target_pairs={{0,16},{16,0},{32,48},{48,32},{64,80},{80,64},{96,112},{112,96},{1... | collective-permute-start | bytes 1572872 | tf_op jit(solution)/shard_map/ppermute | solution.py:31
  35.6 1.5 %shard_map.49 = bf16[16,16,1024]{2,1,0:T(8,128)(2,1)S(1)} custom-call(bf16[128,2688]{1,0:T(8,128)(2,1)S(1)} %collective-permute-done.refs_4_.refs_0_.refs_3_, bf16[16,1536]{1,0:T(8,128)(2,1)S(1)} %pad_maximum_fusion.1.refs_1_, bf16[128,1536]{1,0:T(8,128)(2,1)S(1)} %get-tuple-element.10.refs_2_, bf16[128,1536]{1,0:T(8,128)(2,1)S(1)} %collective-permute-done.1.refs_3_.refs_4_, ...), custom_call_target="tpu_custom_call" | custom-call | flops 805306368 | bytes 1179648 | tf_op jit(solution)/shard_map/pallas_call | solution.py:137
  37.1 0.2 add_convert_fusion
  37.3 18.9 %all_to_all.5 = bf16[16,16,1024]{2,1,0:T(8,128)(2,1)S(1)} all-to-all(bf16[16,16,1024]{2,1,0:T(8,128)(2,1)S(1)} %add_convert_fusion), channel_id=1, replica_groups={{0,32,64,96,128,160,192,224,256,288,320,352,384,416,448,480},{16,48,80,..., dimensions={0} | all-to-all | bytes 1048576 | tf_op jit(solution)/shard_map/all_to_all | solution.py:198
  56.2 0.1 convert_reduce_fusion
  56.3 1.9 %collective-permute-start.5 = (f32[16,1024]{1,0:T(8,128)S(1)}, f32[16,1024]{1,0:T(8,128)S(1)}, u32[]{:S(2)}, u32[]{:S(2)}) collective-permute-start(f32[16,1024]{1,0:T(8,128)S(1)} %convert_reduce_fusion), channel_id=1, source_target_pairs={{1,0},{2,1},{3,2},{4,3},{5,4},{6,5},{7,6},{8,7},{9,8},{10,9},{11,1... | collective-permute-start | bytes 196616 | tf_op jit(solution)/shard_map/ppermute | solution.py:27
  58.2 5.6 %collective-permute-done.5 = f32[16,1024]{1,0:T(8,128)S(1)} collective-permute-done((f32[16,1024]{1,0:T(8,128)S(1)}, f32[16,1024]{1,0:T(8,128)S(1)}, u32[]{:S(2)}, u32[]{:S(2)}) %collective-permute-start.5) | collective-permute-done | bytes 65568 | tf_op jit(solution)/shard_map/ppermute | solution.py:27
  63.9 1.9 %collective-permute-start.6 = (f32[2,4,1024]{2,1,0:T(4,128)S(1)}, f32[2,4,1024]{2,1,0:T(4,128)S(1)}, u32[]{:S(2)}, u32[]{:S(2)}) collective-permute-start(f32[2,4,1024]{2,1,0:T(4,128)S(1)} %fusion.8), channel_id=1, source_target_pairs={{0,16},{16,0},{32,48},{48,32},{64,80},{80,64},{96,112},{112,96},{1... | collective-permute-start | bytes 98312 | tf_op jit(solution)/shard_map/ppermute | solution.py:31
  65.8 1.2 %collective-permute-done.6 = f32[2,4,1024]{2,1,0:T(4,128)S(1)} collective-permute-done((f32[2,4,1024]{2,1,0:T(4,128)S(1)}, f32[2,4,1024]{2,1,0:T(4,128)S(1)}, u32[]{:S(2)}, u32[]{:S(2)}) %collective-permute-start.6) | collective-permute-done | bytes 32800 | tf_op jit(solution)/shard_map/ppermute | solution.py:31
  67.0 0.7 %maximum_multiply_fusion = f32[1,4,4,1024]{3,2,1,0:T(4,128)} fusion(f32[1,2,4,1024]{3,2,1,0:T(4,128)S(1)} %reverse_bitcast_fusion, f32[1,2,4,1024]{3,2,1,0:T(4,128)S(1)} %get-tuple-element.13, f32[4]{0:T(128)S(1)} %multiply_bitcast_fusion), kind=kLoop, calls=%fused_computation.16 | loop fusion | flops 32768 | bytes 131088 | tf_op jit(solution)/shard_map/mul | solution.py:208
  (18 shorter events, 0.1 us)
Async XLA Ops:
  0.7 0.7 copy-start.1
  1.3 1.2 %copy-start = (bf16[1,1,128,4096]{3,2,1,0:T(8,128)(2,1)S(1)}, bf16[1,1,128,4096]{3,2,1,0:T(8,128)(2,1)}, u32[]{:S(2)}) copy-start(bf16[1,1,128,4096]{3,2,1,0:T(8,128)(2,1)} %param.4) | copy-start | bytes 3145732
  2.8 20.1 %collective-permute-start = (bf16[128,2688]{1,0:T(8,128)(2,1)S(1)}, bf16[128,2688]{1,0:T(8,128)(2,1)S(1)}, u32[]{:S(2)}, u32[]{:S(2)}) collective-permute-start(bf16[128,2688]{1,0:T(8,128)(2,1)S(1)} %get-tuple-element.9.refs_2_), channel_id=1, source_target_pairs={{0,1},{1,2},{2,3},{3,4},{4,5},{5,6},{6,7},{7,8},{8,9},{9,10},{10,1... | collective-permute-start | bytes 2064392 | tf_op jit(solution)/shard_map/ppermute | solution.py:27
  7.9 19.6 %collective-permute-start.3 = (bf16[128,2688]{1,0:T(8,128)(2,1)S(1)}, bf16[128,2688]{1,0:T(8,128)(2,1)S(1)}, u32[]{:S(2)}, u32[]{:S(2)}) collective-permute-start(bf16[128,2688]{1,0:T(8,128)(2,1)S(1)} %get-tuple-element.9.refs_2_), channel_id=1, source_target_pairs={{1,0},{2,1},{3,2},{4,3},{5,4},{6,5},{7,6},{8,7},{9,8},{10,9},{11,1... | collective-permute-start | bytes 2064392 | tf_op jit(solution)/shard_map/ppermute | solution.py:27
  9.8 21.8 %collective-permute-start.1 = (bf16[128,1536]{1,0:T(8,128)(2,1)S(1)}, bf16[128,1536]{1,0:T(8,128)(2,1)S(1)}, u32[]{:S(2)}, u32[]{:S(2)}) collective-permute-start(bf16[128,1536]{1,0:T(8,128)(2,1)S(1)} %get-tuple-element.10.refs_2_), channel_id=1, source_target_pairs={{0,1},{1,2},{2,3},{3,4},{4,5},{5,6},{6,7},{7,8},{8,9},{9,10},{10,1... | collective-permute-start | bytes 1179656 | tf_op jit(solution)/shard_map/ppermute | solution.py:27
  14.9 16.8 %collective-permute-start.2 = (bf16[128,1536]{1,0:T(8,128)(2,1)S(1)}, bf16[128,1536]{1,0:T(8,128)(2,1)S(1)}, u32[]{:S(2)}, u32[]{:S(2)}) collective-permute-start(bf16[128,1536]{1,0:T(8,128)(2,1)S(1)} %get-tuple-element.10.refs_2_), channel_id=1, source_target_pairs={{1,0},{2,1},{3,2},{4,3},{5,4},{6,5},{7,6},{8,7},{9,8},{10,9},{11,1... | collective-permute-start | bytes 1179656 | tf_op jit(solution)/shard_map/ppermute | solution.py:27
  33.2 3.9 %collective-permute-start.4 = (bf16[16,16,1024]{2,1,0:T(8,128)(2,1)S(1)}, bf16[16,16,1024]{2,1,0:T(8,128)(2,1)S(1)}, u32[]{:S(2)}, u32[]{:S(2)}) collective-permute-start(bf16[16,16,1024]{2,1,0:T(8,128)(2,1)S(1)} %shard_map.50), channel_id=1, source_target_pairs={{0,16},{16,0},{32,48},{48,32},{64,80},{80,64},{96,112},{112,96},{1... | collective-permute-start | bytes 1572872 | tf_op jit(solution)/shard_map/ppermute | solution.py:31
  56.3 7.5 %collective-permute-start.5 = (f32[16,1024]{1,0:T(8,128)S(1)}, f32[16,1024]{1,0:T(8,128)S(1)}, u32[]{:S(2)}, u32[]{:S(2)}) collective-permute-start(f32[16,1024]{1,0:T(8,128)S(1)} %convert_reduce_fusion), channel_id=1, source_target_pairs={{1,0},{2,1},{3,2},{4,3},{5,4},{6,5},{7,6},{8,7},{9,8},{10,9},{11,1... | collective-permute-start | bytes 196616 | tf_op jit(solution)/shard_map/ppermute | solution.py:27
  63.8 2.0 %copy-start.2 = (s32[1,4]{1,0:T(1,128)S(1)}, s32[1,4]{1,0:T(1,128)}, u32[]{:S(2)}) copy-start(s32[1,4]{1,0:T(1,128)} %param.6) | copy-start | bytes 52
  63.9 3.1 %collective-permute-start.6 = (f32[2,4,1024]{2,1,0:T(4,128)S(1)}, f32[2,4,1024]{2,1,0:T(4,128)S(1)}, u32[]{:S(2)}, u32[]{:S(2)}) collective-permute-start(f32[2,4,1024]{2,1,0:T(4,128)S(1)} %fusion.8), channel_id=1, source_target_pairs={{0,16},{16,0},{32,48},{48,32},{64,80},{80,64},{96,112},{112,96},{1... | collective-permute-start | bytes 98312 | tf_op jit(solution)/shard_map/ppermute | solution.py:31
